TPU v7x, 768 devices: a whole 4x8x12 slice. The times are simulated.
768 devices in a mesh: rows: 12 (over z), cols: 8 (over y_hi, core), poles: 8 (over x, y_lo).
Axes of the slice: x: 4, y: 8 (y_hi: 4, y_lo: 2; y = y_hi * 2 + y_lo), z: 12, core: 2. Of those that a mesh axis runs over, the one named last changes fastest.
Arguments:
- inverse_grid: float32 [8, 12, 128, 8, 192], P('poles', 'rows', None, 'cols'), may hold values from -6 to 6
- factor_b: float32 [8, 12, 8, 16, 512], P('poles', 'rows', 'cols'), may hold values from -0.15625 to 0.15625
- factor_a: float32 [8, 12, 8, 16, 512], P('poles', 'rows', 'cols'), may hold values from -0.15625 to 0.15625
- coupling_a: float32 [8, 512, 512], P('poles'), may hold values from -0.25 to 0.25
- diag_inv_b: float32 [8, 512, 512], P('poles'), may hold values from -6 to 6
- diag_inv_a: float32 [8, 512, 512], P('poles'), may hold values from -6 to 6
- pole_weights: float32 [8], P('poles'), may hold values from 0.1 to 0.6
- structure: int32 [2, 12, 8], P(None, 'rows', 'cols'), may hold values 0 or 1
Outputs:
- density_panel: float32 [12, 8, 16, 512], P('rows', 'cols', None, 'poles')
- density_diag: float32 [512, 512], P('poles', 'cols')
All inputs are finite; a program needn't handle non-finite values. No bound on the sum of `structure` on one device may be relied on, other than what follows from the above.
Results may differ from a plain program's by a relative error of at most 0.00008.
Values sent between devices are 32-bit elements; how exact they have to be, the bound alone decides.
A program may use at most 32 MiB of HBM per device.

v0:
```python
import jax
import jax.numpy as jnp
from jax import lax
from jax.sharding import PartitionSpec as P


def sent_together(arrays, axis, dim, along):
    both = jnp.concatenate(arrays, axis=along)
    whole, at, done = (lax.all_gather(both, axis, axis=dim, tiled=True), 0, [])
    for a in arrays:
        done.append(lax.slice_in_dim(whole, at, at + a.shape[along], axis=along))
        at += a.shape[along]
    return tuple(done)


def split_up(array, dim, count):
    dims = array.shape
    tiles = array.reshape(*dims[:dim], count, dims[dim] // count, *dims[dim + 1 :])
    return jnp.moveaxis(tiles, dim, 0)


def sent_and_summed(array, axis, dim):
    tiles = split_up(array, dim, lax.axis_size(axis))
    arrived = lax.all_to_all(tiles, axis, split_axis=0, concat_axis=0, tiled=True)
    return arrived.sum(axis=0)


def in_one_piece(arrays, axis, dim, along):
    both = jnp.concatenate(arrays, axis=along)
    whole, at, done = (sent_and_summed(both, axis, dim), 0, [])
    for a in arrays:
        done.append(lax.slice_in_dim(whole, at, at + a.shape[along], axis=along))
        at += a.shape[along]
    return tuple(done)


def copy_for_each(array, axis):
    count = lax.axis_size(axis)
    return lax.all_to_all(
        jnp.broadcast_to(array[None], (count, *array.shape)), axis, 0, 0, tiled=True
    )


def taken_together(array, axis):
    everything = copy_for_each(array, axis)
    return jnp.sum(everything, axis=0)


def product(left, right):
    return jnp.dot(left, right, precision=lax.Precision.HIGHEST, preferred_element_type=jnp.float32)


def shards(
    inverse_grid, factor_b, factor_a, coupling_a, diag_inv_b, diag_inv_a, pole_weights, structure
):
    local_grid = inverse_grid[0, 0, :, 0, :]
    kept_mask = structure[:, 0, 0].astype(jnp.float32)
    panel_b = factor_b[0, 0, 0] * kept_mask[0]
    panel_a = factor_a[0, 0, 0] * kept_mask[1]
    coupling = coupling_a[0]
    inv_diag_b = diag_inv_b[0]
    inv_diag_a = diag_inv_a[0]
    weight = pole_weights[0]
    pieces = sent_together((panel_b, panel_a), "rows", 0, 1)
    part_b = product(local_grid, pieces[0])
    part_a = product(local_grid, pieces[1])
    summed_b, summed_a = in_one_piece((part_b, part_a), "cols", 0, 1)
    inv_b = -summed_b
    inv_as = -(product(inv_b, coupling) + summed_a)
    owned_part = inv_diag_a + product(product(coupling.T, inv_diag_b), coupling)
    local_extra = product(
        coupling.T, product(inv_b.T, panel_a) - product(product(panel_b.T, inv_b), coupling)
    )
    leader = jnp.logical_and(lax.axis_index("rows") == 0, lax.axis_index("cols") == 0)
    diag_term = weight * (
        jnp.where(leader, owned_part, jnp.zeros_like(owned_part))
        + local_extra
        - product(panel_a.T, inv_as)
    )
    panel_sum = sent_and_summed(weight * inv_as, "poles", 1)
    pole_part = sent_and_summed(diag_term, "poles", 0)
    column_share = sent_and_summed(pole_part, "cols", 1)
    density_diag = taken_together(column_share, "rows")
    return (panel_sum[None, None], density_diag)


def solution(mesh):
    in_specs = (
        P("poles", "rows", None, "cols", None),
        P("poles", "rows", "cols", None, None),
        P("poles", "rows", "cols", None, None),
        P("poles", None, None),
        P("poles", None, None),
        P("poles", None, None),
        P("poles"),
        P(None, "rows", "cols"),
    )
    out_specs = (P("rows", "cols", None, "poles"), P("poles", "cols"))
    return jax.shard_map(shards, mesh=mesh, in_specs=in_specs, out_specs=out_specs, check_vma=False)
```

profile of v0, /device:TPU:8, one launch (start us, length us, event | category | flops | bytes accessed | tf_op | source)
XLA Modules:
  0.0 136.3 jit_solution(1162857776887215390)
XLA Ops:
  0.6 0.7 convert_element_type.4
  1.4 0.6 fusion.17
  2.0 2.1 %multiply_bitcast_fusion = (f32[16,512]{1,0:T(8,128)S(1)}, f32[16,512]{1,0:T(8,128)S(1)}) fusion(f32[1,1,1,16,512]{4,3,2,1,0:T(8,128)} %param.10, f32[]{:T(128)} %bitcast.3, f32[1,1,1,16,512]{4,3,2,1,0:T(8,128)} %param.9, f32[]{:T(128)} %bitcast.1), kind=kLoop, calls=%fused_computation.26 | loop fusion | flops 16384 | bytes 131080 | tf_op jit(solution)/shard_map/mul | solution.py:59
  4.1 37.3 %all_gather.3 = f32[192,1024]{1,0:T(8,128)S(1)} all-gather(f32[16,1024]{1,0:T(8,128)S(1)} %pad_maximum_fusion.1), channel_id=1, replica_groups=mesh['rows'=12,'cols'=8,'poles'=8] {'rows'}, dimensions={0}, use_global_device_ids=true | all-gather | bytes 851968 | tf_op jit(solution)/shard_map/all_gather | solution.py:9
  41.3 1.1 convolution_bitcast_fusion.1
  42.4 1.1 convolution_bitcast_fusion.2
  43.5 1.0 copy.16
  44.5 6.3 %all-to-all-start = ((f32[8,16,1024]{2,1,0:T(8,128)}), f32[8,16,1024]{2,1,0:T(8,128)S(1)}, u32[]{:S(2)}, u32[]{:S(2)}) async-start(f32[8,16,1024]{2,1,0:T(8,128)} %bitcast.8), calls=%async_computation | async-start | bytes 1048576 | tf_op jit(solution)/shard_map/all_to_all | solution.py:24
  51.6 1.8 %fusion.4 = f32[512,512]{1,0:T(8,128)S(1)} fusion(f32[1,512,512]{2,1,0:T(8,128)S(1)} %copy-done.1, f32[1,512,512]{2,1,0:T(8,128)S(1)} %copy-done), kind=kOutput, calls=%fused_computation.11 | convolution fusion | flops 1610612736 | bytes 3145728 | tf_op jit(solution)/shard_map/dot_general | solution.py:50
  53.4 1.9 %fusion.2 = f32[512,512]{1,0:T(8,128)S(1)} fusion(f32[512,512]{1,0:T(8,128)S(1)} %fusion.4, f32[1,512,512]{2,1,0:T(8,128)S(1)} %copy-done.2, f32[1,512,512]{2,1,0:T(8,128)S(1)} %copy-done, pred[]{:T(512)S(6)} %and.4), kind=kOutput, calls=%fused_computation.6 | convolution fusion | flops 1611137024 | bytes 4194305 | tf_op jit(solution)/shard_map/dot_general | solution.py:50
  55.3 12.3 %all-to-all-done = f32[8,16,1024]{2,1,0:T(8,128)S(1)} async-done(((f32[8,16,1024]{2,1,0:T(8,128)}), f32[8,16,1024]{2,1,0:T(8,128)S(1)}, u32[]{:S(2)}, u32[]{:S(2)}) %all-to-all-start) | async-done | bytes 524320 | tf_op jit(solution)/shard_map/all_to_all | solution.py:24
  67.6 1.0 fusion.15
  68.7 1.0 fusion.16
  69.7 0.6 broadcast_multiply_fusion
  70.3 1.9 %convolution_subtract_fusion.1 = f32[512,512]{1,0:T(8,128)S(1)} fusion(f32[512,512]{1,0:T(8,128)S(1)} %fusion.16, f32[512,512]{1,0:T(8,128)S(1)} %fusion.15, f32[1,512,512]{2,1,0:T(8,128)S(1)} %copy-done), kind=kOutput, calls=%fused_computation.4 | convolution fusion | flops 1610874880 | bytes 4194304 | tf_op jit(solution)/shard_map/dot_general | solution.py:50
  72.2 1.9 %fusion.1 = f32[512,512]{1,0:T(8,128)S(1)} fusion(f32[512,512]{1,0:T(8,128)S(1)} %fusion.2, f32[512,512]{1,0:T(8,128)S(1)} %convolution_subtract_fusion.1, f32[1,512,512]{2,1,0:T(8,128)S(1)} %copy-done), kind=kOutput, calls=%fused_computation.3 | convolution fusion | flops 1610874880 | bytes 4194304 | tf_op jit(solution)/shard_map/dot_general | solution.py:50
  74.1 1.1 fusion
  75.1 19.3 %all_to_all.25 = f32[8,64,512]{2,1,0:T(8,128)S(1)} all-to-all(f32[8,64,512]{2,1,0:T(8,128)S(1)} %bitcast.54), channel_id=1, replica_groups=mesh['rows'=12,'cols'=8,'poles'=8] {'poles'}, dimensions={0} | all-to-all | bytes 2097152 | tf_op jit(solution)/shard_map/all_to_all | solution.py:24
  94.6 0.8 reshape.32
  95.5 3.4 %all-to-all-start.3 = ((f32[8,1,4096]{2,1,0:T(1,128)}), f32[8,1,4096]{2,1,0:T(1,128)S(1)}, u32[]{:S(2)}, u32[]{:S(2)}) async-start(f32[8,1,4096]{2,1,0:T(1,128)} %reshape.32), calls=%async_computation.3 | async-start | bytes 262144 | tf_op jit(solution)/shard_map/all_to_all | solution.py:24
  98.9 0.7 reshape.30
  99.6 8.8 %all-to-all-done.3 = f32[8,1,4096]{2,1,0:T(1,128)S(1)} async-done(((f32[8,1,4096]{2,1,0:T(1,128)}), f32[8,1,4096]{2,1,0:T(1,128)S(1)}, u32[]{:S(2)}, u32[]{:S(2)}) %all-to-all-start.3) | async-done | bytes 131104 | tf_op jit(solution)/shard_map/all_to_all | solution.py:24
  108.5 3.7 %all-to-all-start.1 = ((f32[8,1,1024]{2,1,0:T(1,128)}), f32[8,1,1024]{2,1,0:T(1,128)S(1)}, u32[]{:S(2)}, u32[]{:S(2)}) async-start(f32[8,1,1024]{2,1,0:T(1,128)} %reshape.30), calls=%async_computation.1 | async-start | bytes 65536 | tf_op jit(solution)/shard_map/all_to_all | solution.py:24
  112.8 0.9 reduce.1
  113.9 0.9 reshape.34
  114.8 2.3 %all-to-all-done.1 = f32[8,1,1024]{2,1,0:T(1,128)S(1)} async-done(((f32[8,1,1024]{2,1,0:T(1,128)}), f32[8,1,1024]{2,1,0:T(1,128)S(1)}, u32[]{:S(2)}, u32[]{:S(2)}) %all-to-all-start.1) | async-done | bytes 32800 | tf_op jit(solution)/shard_map/all_to_all | solution.py:24
  117.1 3.5 %all-to-all-start.4 = ((f32[12,1,4096]{2,1,0:T(1,128)}), f32[12,1,4096]{2,1,0:T(1,128)S(1)}, u32[]{:S(2)}, u32[]{:S(2)}) async-start(f32[12,1,4096]{2,1,0:T(1,128)} %reshape.34), calls=%async_computation.4 | async-start | bytes 393216 | tf_op jit(solution)/shard_map/all_to_all | solution.py:39
  120.6 0.7 reduce
  121.4 0.6 reduce_sum.46
  122.0 12.4 %all-to-all-done.4 = f32[12,1,4096]{2,1,0:T(1,128)S(1)} async-done(((f32[12,1,4096]{2,1,0:T(1,128)}), f32[12,1,4096]{2,1,0:T(1,128)S(1)}, u32[]{:S(2)}, u32[]{:S(2)}) %all-to-all-start.4) | async-done | bytes 196640 | tf_op jit(solution)/shard_map/all_to_all | solution.py:39
  134.4 1.1 reduce.2
  135.7 0.7 reduce_sum.49
  (22 shorter events, 1.4 us)
Async XLA Ops:
  0.6 50.9 %copy-start = (f32[1,512,512]{2,1,0:T(8,128)S(1)}, f32[1,512,512]{2,1,0:T(8,128)}, u32[]{:S(2)}) copy-start(f32[1,512,512]{2,1,0:T(8,128)} %param.11) | copy-start | bytes 3145732
  4.1 37.3 %copy-start.3 = (f32[1,1,128,1,192]{2,4,3,1,0:T(8,128)S(1)}, f32[1,1,128,1,192]{2,4,3,1,0:T(8,128)}, u32[]{:S(2)}) copy-start(f32[1,1,128,1,192]{2,4,3,1,0:T(8,128)} %param.8) | copy-start | bytes 294916
  44.5 7.0 %copy-start.1 = (f32[1,512,512]{2,1,0:T(8,128)S(1)}, f32[1,512,512]{2,1,0:T(8,128)}, u32[]{:S(2)}) copy-start(f32[1,512,512]{2,1,0:T(8,128)} %param.12) | copy-start | bytes 3145732
  44.5 23.0 %all-to-all-start = ((f32[8,16,1024]{2,1,0:T(8,128)}), f32[8,16,1024]{2,1,0:T(8,128)S(1)}, u32[]{:S(2)}, u32[]{:S(2)}) async-start(f32[8,16,1024]{2,1,0:T(8,128)} %bitcast.8), calls=%async_computation | async-start | bytes 1048576 | tf_op jit(solution)/shard_map/all_to_all | solution.py:24
  51.5 1.9 %copy-start.2 = (f32[1,512,512]{2,1,0:T(8,128)S(1)}, f32[1,512,512]{2,1,0:T(8,128)}, u32[]{:S(2)}) copy-start(f32[1,512,512]{2,1,0:T(8,128)} %param.13) | copy-start | bytes 3145732
  95.5 13.0 %all-to-all-start.3 = ((f32[8,1,4096]{2,1,0:T(1,128)}), f32[8,1,4096]{2,1,0:T(1,128)S(1)}, u32[]{:S(2)}, u32[]{:S(2)}) async-start(f32[8,1,4096]{2,1,0:T(1,128)} %reshape.32), calls=%async_computation.3 | async-start | bytes 262144 | tf_op jit(solution)/shard_map/all_to_all | solution.py:24
  108.5 8.6 %all-to-all-start.1 = ((f32[8,1,1024]{2,1,0:T(1,128)}), f32[8,1,1024]{2,1,0:T(1,128)S(1)}, u32[]{:S(2)}, u32[]{:S(2)}) async-start(f32[8,1,1024]{2,1,0:T(1,128)} %reshape.30), calls=%async_computation.1 | async-start | bytes 65536 | tf_op jit(solution)/shard_map/all_to_all | solution.py:24
  117.1 17.3 %all-to-all-start.4 = ((f32[12,1,4096]{2,1,0:T(1,128)}), f32[12,1,4096]{2,1,0:T(1,128)S(1)}, u32[]{:S(2)}, u32[]{:S(2)}) async-start(f32[12,1,4096]{2,1,0:T(1,128)} %reshape.34), calls=%async_computation.4 | async-start | bytes 393216 | tf_op jit(solution)/shard_map/all_to_all | solution.py:39
where the time goes:
time: 137 us; the launch traced here: 136 us
  blocking collectives  56.5 us (41%)
  waiting for transfers between devices  35.9 us (26%)
  starting transfers between devices  16.9 us (12%)
  matrix products  13.3 us (10%)
  other arithmetic  6.97 us (5%)
  local copies, waits for them, and re-layouts  5.22 us (4%)
  between operations  1.5 us (1%)
    all_gather x1, blocking collectives, sent_together(): whole, at, done = (lax.all_gather(both, axis, axis=dim, tiled=True), 0, [])  37.3 us
    all_to_all x3, waiting for transfers between devices, sent_and_summed(): lax.all_to_all(tiles, axis, split_axis=0, concat_axis=0, tiled=True)  23.5 us
    all_to_all x1, blocking collectives, sent_and_summed(): lax.all_to_all(tiles, axis, split_axis=0, concat_axis=0, tiled=True)  19.3 us
    all_to_all x3, starting transfers between devices, sent_and_summed(): lax.all_to_all(tiles, axis, split_axis=0, concat_axis=0, tiled=True)  13.4 us
    dot_general x10, matrix products, product(): jnp.dot(left, right, precision=lax.Precision.HIGHEST, preferred_element_t...  13.3 us
    all_to_all x1, waiting for transfers between devices, copy_for_each(): lax.all_to_all(jnp.broadcast_to(array[None], (count, *array.shape)), axis...  12.4 us
    all_to_all x1, starting transfers between devices, copy_for_each(): lax.all_to_all(jnp.broadcast_to(array[None], (count, *array.shape)), axis...  3.53 us
    unnamed x14, local copies, waits for them, and re-layouts  2.8 us
  transfers between devices with their start and end apart: 4, of which 4 were waited for; matrix products, arithmetic and copies ran while one was open for 6% of the time, Pallas kernels for 0%

commit v1 on v0

v1 whole, which is shorter than its diff:
```python
import jax
import jax.numpy as jnp
from jax import lax
from jax.experimental import pallas as pl
from jax.experimental.pallas import tpu as pltpu
from jax.sharding import PartitionSpec as P

MESH = pl.DeviceIdType.MESH
F32 = jnp.float32
WIDTH, BLOCK = 512, 16
NR, NC, NP = 12, 8, 8
CHUNK = WIDTH // NP
LANES = 2 * CHUNK
ROWS = NC * BLOCK
PER_CORE = NC // 2
HALF = CHUNK // 2
RIGHT_REACH = (6, 5)
LEFT_REACH = (5, 6)


def dot(left, right, contract=((1,), (0,))):
    return lax.dot_general(
        left, right, (contract, ((), ())), precision=lax.Precision.HIGH, preferred_element_type=F32
    )


def swap_halves(x):
    return pltpu.roll(x, CHUNK, axis=x.ndim - 1)


def low_lanes(shape):
    return lax.broadcasted_iota(jnp.int32, shape, len(shape) - 1) < CHUNK


def pack(top, bottom):
    return jnp.where(low_lanes(top.shape), top, swap_halves(bottom))


def unpack(x):
    return jnp.concatenate([x, swap_halves(x)], axis=0)


def remote(src, dst, send, recv, to):
    return pltpu.make_async_remote_copy(
        src_ref=src, dst_ref=dst, send_sem=send, recv_sem=recv, device_id=to, device_id_type=MESH
    )


def kernel(
    g_hbm, lb_hbm, la_hbm, c_hbm, db_hbm, da_hbm, weight_s, keep_s,
    panel_ref, diag_ref,
    gt, lb, la, coup, dbk, dak, own, zbuf, rows, wsend, wrecv, fsend, frecv, qsend, qrecv, tsend, trecv,
    load_sem, g_send, g_recv, z_send, z_recv, hop_send, pair_send, pair_recv, r_send, r_recv,
    w_send, w_recv, f_send, f_recv, q_send, q_recv, t_send, t_recv,
):
    u, v, p = lax.axis_index("rows"), lax.axis_index("cols"), lax.axis_index("poles")
    h, chip = lax.rem(v, 2), v // 2
    mate = chip * 2 + 1 - h
    part = jnp.minimum(u, NP - 1)

    loads = [
        pltpu.make_async_copy(lb_hbm, lb, load_sem.at[0]),
        pltpu.make_async_copy(la_hbm, la, load_sem.at[1]),
        pltpu.make_async_copy(c_hbm, coup, load_sem.at[2]),
        pltpu.make_async_copy(g_hbm, gt.at[h], load_sem.at[3]),
        pltpu.make_async_copy(db_hbm.at[pl.ds(part * CHUNK, CHUNK)], dbk, load_sem.at[4]),
        pltpu.make_async_copy(da_hbm.at[pl.ds(v * CHUNK, CHUNK)], dak, load_sem.at[5]),
    ]
    for copy in loads:
        copy.start()

    barrier = pltpu.get_barrier_semaphore()

    def greet(to):
        pl.semaphore_signal(barrier, inc=1, device_id=to, device_id_type=MESH)

    for step in (1, NR - 1):
        greet((lax.rem(u + step, NR), mate, p))
    for step in range(1, NR):
        greet((lax.rem(u + step, NR), v, p))
    for step in range(1, NC):
        greet((u, lax.rem(v + step, NC), p))
        greet((u, v, lax.rem(p + step, NP)))
    for q in range(NP):

        @pl.when(jnp.logical_not(jnp.logical_and(v == p, p == q)))
        def _():
            greet((u, p, q))

    weight = weight_s[0]
    keep_b = keep_s[0].astype(F32)
    keep_a = keep_s[1].astype(F32)
    for copy in loads[:3]:
        copy.wait()
    panel_a = la[...] * keep_a
    panel_n = dot(lb[...] * keep_b, coup[...])
    for pair in range(NC // 2):
        a, n = (x[:, pair * LANES : (pair + 1) * LANES] for x in (panel_a, panel_n))
        own[2 * pair] = pack(a, n)
        own[2 * pair + 1] = jnp.where(low_lanes(a.shape), swap_halves(a), n)
    loads[3].wait()

    expected = 2 + (NR - 1) + (NC - 1) + (NP - 1) + NP
    pl.semaphore_wait(barrier, expected - (v == p).astype(jnp.int32))

    right, left = lax.rem(u + 1, NR), lax.rem(u + NR - 1, NR)
    mine = own.at[pl.ds(h * PER_CORE, PER_CORE)]
    others = own.at[pl.ds((1 - h) * PER_CORE, PER_CORE)]
    sent = []

    def send(copy):
        copy.start()
        sent.append(copy)

    for d, to in ((0, right), (1, left)):
        send(remote(mine, zbuf.at[h, u], hop_send.at[d, 0], z_recv.at[d, 0, h], (to, v, p)))
        send(remote(others, zbuf.at[h, u], hop_send.at[d, 1], z_recv.at[d, 0, h], (to, mate, p)))
    send(remote(others, zbuf.at[h, u], pair_send, pair_recv, (u, mate, p)))
    send(remote(gt.at[h], gt.at[h], g_send, g_recv, (u, mate, p)))
    for step in range(1, NC):
        to = lax.rem(v + step, NC)
        send(remote(own, rows.at[v], r_send.at[step - 1], r_recv.at[v], (u, to, p)))
    zbuf[h, u] = own[pl.ds(h * PER_CORE, PER_CORE)]
    rows[v] = own[...]

    for copy in loads[4:]:
        copy.wait()
    columns = coup[:, pl.ds(pl.multiple_of(chip * LANES, LANES), LANES)]
    inner = dot(dbk[...], columns)
    inner = jnp.where(h == 0, inner, swap_halves(inner))
    inner = inner * (weight * (u < NP).astype(F32))
    fixed = dot(inner, coup[pl.ds(part * CHUNK, CHUNK), :], ((0,), (0,)))[:CHUNK]

    def arrived(buf, sem):
        remote(buf, buf, pair_send, sem, (u, mate, p)).wait_recv()

    for hop in range(1, NR // 2 + 1):
        for s in range(2):
            for d, (reach, to) in enumerate(((RIGHT_REACH, right), (LEFT_REACH, left))):
                if hop > reach[s]:
                    continue
                origin = lax.rem(u + (NR - hop if d == 0 else hop), NR)
                slot = zbuf.at[s, origin]
                arrived(slot, z_recv.at[d, hop - 1, s])
                if hop < reach[s]:
                    send(remote(slot, slot, z_send.at[d, hop - 1, s], z_recv.at[d, hop, s], (to, v, p)))
        if hop == 1:
            arrived(zbuf.at[1 - h, u], pair_recv)
            arrived(gt.at[1 - h], g_recv)
            inverse = gt[...].reshape(2 * NR * BLOCK, ROWS).T

    for ch in range(PER_CORE):
        gathered = zbuf[:, :, ch].reshape(2 * NR * BLOCK, LANES)
        wsend[ch] = dot(inverse, gathered)
        dest = h * PER_CORE + ch

        @pl.when(dest == v)
        def _():
            wrecv[chip] = wsend[ch]

        @pl.when(dest != v)
        def _():
            remote(wsend.at[ch], wrecv.at[chip], w_send.at[ch], w_recv.at[chip], (u, dest, p)).start()

    for step in range(1, NC):
        source = lax.rem(v + step, NC)
        arrived(rows.at[source], r_recv.at[source])
    for k in range(NC // 2):

        @pl.when(2 * k + v // PER_CORE != v)
        def _():
            arrived(wrecv.at[k], w_recv.at[k])

    both = (wrecv[0] + wrecv[1]) + (wrecv[2] + wrecv[3])
    panel = ((swap_halves(both) - both) * weight).reshape(NC, BLOCK, LANES)
    panel = pack(panel[:, : BLOCK // 2], panel[:, BLOCK // 2 :])
    turned = (both * weight).T
    for a in range(NP):
        terms = dot(turned, rows[:, a].reshape(ROWS, LANES))
        top, bottom = terms[:CHUNK], terms[CHUNK:]
        pair = slice(a // 2 * LANES, (a // 2 + 1) * LANES)
        here, block = fixed[:, pair], dak[:, pair]
        if a % 2:
            here, block = swap_halves(here), swap_halves(block)
        first = (top - bottom) + swap_halves(bottom) + here
        second = block * (weight * (u == a).astype(F32)) - bottom
        fsend[a] = pack(first[:HALF], first[HALF:])
        qsend[a, :HALF] = pack(second[:HALF], second[HALF:])
        qsend[a, HALF:] = panel[a]

        @pl.when(a == p)
        def _():
            frecv[p] = fsend[a]

        @pl.when(a != p)
        def _():
            remote(fsend.at[a], frecv.at[p], f_send.at[a], f_recv.at[p], (u, v, a)).start()

        mine_too = jnp.logical_and(v == p, a == v)

        @pl.when(mine_too)
        def _():
            qrecv[p] = qsend[a]

        @pl.when(jnp.logical_not(mine_too))
        def _():
            remote(qsend.at[a], qrecv.at[p], q_send.at[a], q_recv.at[p], (u, a, v)).start()

    for q in range(NP):

        @pl.when(q != p)
        def _():
            arrived(frecv.at[q], f_recv.at[q])

        @pl.when(jnp.logical_not(jnp.logical_and(v == p, q == p)))
        def _():
            arrived(qrecv.at[q], q_recv.at[q])

    first, second = frecv[0], qrecv[0]
    for q in range(1, NP):
        first, second = first + frecv[q], second + qrecv[q]
    first = unpack(first)
    first = jnp.concatenate([first, first], axis=0).T[:CHUNK]
    total = first + unpack(second[:HALF])
    tsend[...] = pack(total[:HALF], total[HALF:])
    for step in range(1, NR):
        to = lax.rem(u + step, NR)
        send(remote(tsend, trecv.at[u], t_send.at[step - 1], t_recv.at[u], (to, v, p)))
    trecv[u] = tsend[...]
    panel_ref[...] = unpack(second[HALF:])[:, :CHUNK]

    for step in range(1, NR):
        source = lax.rem(u + step, NR)
        arrived(trecv.at[source], t_recv.at[source])
    total = trecv[0]
    for k in range(1, NR):
        total = total + trecv[k]
    diag_ref[...] = unpack(total)[:, :CHUNK]

    for copy in sent:
        copy.wait_send()
    for ch in range(PER_CORE):

        @pl.when(h * PER_CORE + ch != v)
        def _():
            remote(wsend.at[ch], wsend.at[ch], w_send.at[ch], w_recv.at[0], (u, mate, p)).wait_send()

    for a in range(NP):

        @pl.when(a != p)
        def _():
            remote(fsend.at[a], fsend.at[a], f_send.at[a], f_recv.at[0], (u, mate, p)).wait_send()

        @pl.when(jnp.logical_not(jnp.logical_and(v == p, a == v)))
        def _():
            remote(qsend.at[a], qsend.at[a], q_send.at[a], q_recv.at[0], (u, mate, p)).wait_send()


def shards(
    inverse_grid, factor_b, factor_a, coupling_a, diag_inv_b, diag_inv_a, pole_weights, structure
):
    hbm = pl.BlockSpec(memory_space=pl.ANY)
    smem = pl.BlockSpec(memory_space=pltpu.SMEM)
    vmem = pl.BlockSpec(memory_space=pltpu.VMEM)
    dma = pltpu.SemaphoreType.DMA
    panel, diag = pl.pallas_call(
        kernel,
        out_shape=(
            jax.ShapeDtypeStruct((BLOCK, CHUNK), F32),
            jax.ShapeDtypeStruct((CHUNK, CHUNK), F32),
        ),
        in_specs=[hbm] * 6 + [smem] * 2,
        out_specs=(vmem, vmem),
        scratch_shapes=[
            pltpu.VMEM((2, NR * BLOCK, ROWS), F32),
            pltpu.VMEM((BLOCK, WIDTH), F32),
            pltpu.VMEM((BLOCK, WIDTH), F32),
            pltpu.VMEM((WIDTH, WIDTH), F32),
            pltpu.VMEM((CHUNK, WIDTH), F32),
            pltpu.VMEM((CHUNK, WIDTH), F32),
            pltpu.VMEM((NC, BLOCK, LANES), F32),
            pltpu.VMEM((2, NR, PER_CORE, BLOCK, LANES), F32),
            pltpu.VMEM((NC, NC, BLOCK, LANES), F32),
            pltpu.VMEM((PER_CORE, ROWS, LANES), F32),
            pltpu.VMEM((NC // 2, ROWS, LANES), F32),
            pltpu.VMEM((NP, HALF, LANES), F32),
            pltpu.VMEM((NP, HALF, LANES), F32),
            pltpu.VMEM((NP, HALF + BLOCK // 2, LANES), F32),
            pltpu.VMEM((NP, HALF + BLOCK // 2, LANES), F32),
            pltpu.VMEM((HALF, LANES), F32),
            pltpu.VMEM((NR, HALF, LANES), F32),
            dma((6,)), dma, dma, dma((2, 6, 2)), dma((2, 6, 2)), dma((2, 2)), dma, dma,
            dma((NC - 1,)), dma((NC,)), dma((PER_CORE,)), dma((NC // 2,)),
            dma((NP,)), dma((NP,)), dma((NP,)), dma((NP,)), dma((NR - 1,)), dma((NR,)),
        ],
        compiler_params=pltpu.CompilerParams(collective_id=0, has_side_effects=True),
    )(
        inverse_grid[0, 0, :, 0, :].T,
        factor_b[0, 0, 0],
        factor_a[0, 0, 0],
        coupling_a[0],
        diag_inv_b[0],
        diag_inv_a[0],
        pole_weights,
        structure[:, 0, 0],
    )
    return panel[None, None], diag


def solution(mesh):
    in_specs = (
        P("poles", "rows", None, "cols", None),
        P("poles", "rows", "cols", None, None),
        P("poles", "rows", "cols", None, None),
        P("poles", None, None),
        P("poles", None, None),
        P("poles", None, None),
        P("poles"),
        P(None, "rows", "cols"),
    )
    out_specs = (P("rows", "cols", None, "poles"), P("poles", "cols"))
    return jax.shard_map(shards, mesh=mesh, in_specs=in_specs, out_specs=out_specs, check_vma=False)
```

time: 137 us -> 76.1 us (0.56)
  the two profiles are of different devices: /device:TPU:8 before, /device:TPU:51 now
where the time goes in v1:
time: 76.1 us; the launch traced here: 75.8 us
  Pallas kernels  71.8 us (94%)
  local copies, waits for them, and re-layouts  2.67 us (4%)
  between operations  1.29 us (2%)
    pallas_call x1, Pallas kernels, shards(): pl.pallas_call(kernel, out_shape=(jax.ShapeDtypeStruct((BLOCK, CHUNK), F3...  71.8 us
    unnamed x2, local copies, waits for them, and re-layouts  2.67 us

profile of v1, /device:TPU:51, one launch (start us, length us, event | category | flops | bytes accessed | tf_op | source)
XLA Modules:
  0.0 75.8 jit_solution(18105349359990021694)
XLA Ops:
  1.3 71.8 %shard_map.95 = (f32[16,64]{1,0:T(8,128)}, f32[64,64]{1,0:T(8,128)}) custom-call(f32[192,128]{1,0:T(8,128)} %bitcast.13, f32[16,512]{1,0:T(8,128)} %bitcast.14, f32[16,512]{1,0:T(8,128)} %bitcast.15, f32[512,512]{1,0:T(8,128)} %bitcast.10, f32[512,512]{1,0:T(8,128)} %bitcast.11, f32[512,512]{1,0:T(8,128)} %bitcast.12, f32[1]{0:T(128)S(6)} %copy.12.weight_s, ...), custom_call_target="tpu_custom_call" | custom-call | tf_op jit(solution)/shard_map/pallas_call | solution.py:266
  73.1 1.3 %copy.13 = f32[1,1,16,64]{3,2,1,0:T(8,128)} copy(f32[1,1,16,64]{3,2,1,0:T(8,128)} %bitcast.16) | data formatting | bytes 8192
  74.4 1.4 %copy.14 = f32[64,64]{1,0:T(8,128)} copy(f32[64,64]{1,0:T(8,128)} %get-tuple-element.9) | data formatting | bytes 32768

commit v2 on v1

v2 whole, which is shorter than its diff:
```python
import jax
import jax.numpy as jnp
from jax import lax
from jax.experimental import pallas as pl
from jax.experimental.pallas import tpu as pltpu
from jax.sharding import PartitionSpec as P

MESH = pl.DeviceIdType.MESH
F32 = jnp.float32
WIDTH, BLOCK = 512, 16
NR, NC, NP = 12, 8, 8
CHUNK = WIDTH // NP
LANES = 2 * CHUNK
ROWS = NC * BLOCK
PER_CORE = NC // 2
HALF = CHUNK // 2
DIRECT = 2
REACH = ((6, 5), (5, 6))


def dot(left, right, contract=((1,), (0,))):
    return lax.dot_general(
        left, right, (contract, ((), ())), precision=lax.Precision.HIGH, preferred_element_type=F32
    )


def swap_halves(x):
    return pltpu.roll(x, CHUNK, axis=x.ndim - 1)


def low_lanes(shape):
    return lax.broadcasted_iota(jnp.int32, shape, len(shape) - 1) < CHUNK


def pack(top, bottom):
    return jnp.where(low_lanes(top.shape), top, swap_halves(bottom))


def unpack(x):
    return jnp.concatenate([x, swap_halves(x)], axis=0)


def remote(src, dst, send, recv, to):
    return pltpu.make_async_remote_copy(
        src_ref=src, dst_ref=dst, send_sem=send, recv_sem=recv, device_id=to, device_id_type=MESH
    )


def kernel(
    g_hbm, lb_hbm, la_hbm, c_hbm, db_hbm, da_hbm, weight_hbm, keep_hbm,
    panel_ref, diag_ref,
    weight_s, keep_s, gt, lb, la, coup, dbk, dak, fixed, own, zbuf, rows, turned, wsend, wrecv, fsend, frecv, qsend, qrecv, tsend, trecv,
    load_sem, scalar_sem, g_send, g_recv, z_send, z_recv, hop_send, pair_send, pair_recv, r_send, r_recv,
    w_send, w_recv, f_send, f_recv, q_send, q_recv, t_send, t_recv,
):
    u, v, p = lax.axis_index("rows"), lax.axis_index("cols"), lax.axis_index("poles")
    h, chip = lax.rem(v, 2), v // 2
    mate = chip * 2 + 1 - h
    part = jnp.minimum(u, NP - 1)

    loads = [
        pltpu.make_async_copy(lb_hbm, lb, load_sem.at[0]),
        pltpu.make_async_copy(la_hbm, la, load_sem.at[1]),
        pltpu.make_async_copy(c_hbm, coup, load_sem.at[2]),
        pltpu.make_async_copy(g_hbm, gt.at[h], load_sem.at[3]),
        pltpu.make_async_copy(db_hbm.at[pl.ds(part * CHUNK, CHUNK)], dbk, load_sem.at[4]),
        pltpu.make_async_copy(da_hbm.at[pl.ds(part * CHUNK, CHUNK), pl.ds(pl.multiple_of(chip * LANES, LANES), LANES)], dak, load_sem.at[5]),
    ]
    scalars = [
        pltpu.make_async_copy(weight_hbm, weight_s, scalar_sem.at[0]),
        pltpu.make_async_copy(keep_hbm, keep_s, scalar_sem.at[1]),
    ]
    for copy in loads[:3] + scalars + loads[3:]:
        copy.start()

    barrier = pltpu.get_barrier_semaphore()

    def greet(to):
        pl.semaphore_signal(barrier, inc=1, device_id=to, device_id_type=MESH)

    for step in range(1, DIRECT + 1):
        for to in (lax.rem(u + step, NR), lax.rem(u + NR - step, NR)):
            greet((to, v, p))
            greet((to, mate, p))
    for step in range(1, NC):
        greet((u, lax.rem(v + step, NC), p))
        greet((u, v, lax.rem(p + step, NP)))
    for copy in scalars + loads[:3]:
        copy.wait()
    weight = weight_s[0]
    keep_b = keep_s[0].astype(F32)
    keep_a = keep_s[1].astype(F32)
    panel_a = la[...] * keep_a
    panel_n = dot(lb[...] * keep_b, coup[...])
    for pair in range(NC // 2):
        a, n = (x[:, pair * LANES : (pair + 1) * LANES] for x in (panel_a, panel_n))
        own[2 * pair] = pack(a, n)
        own[2 * pair + 1] = jnp.where(low_lanes(a.shape), swap_halves(a), n)
    loads[3].wait()

    pl.semaphore_wait(barrier, 4 * DIRECT + (NC - 1) + (NP - 1))

    mine = own.at[pl.ds(h * PER_CORE, PER_CORE)]
    others = own.at[pl.ds((1 - h) * PER_CORE, PER_CORE)]
    sent = []

    def send(copy):
        copy.start()
        sent.append(copy)

    def along(d, hops):
        return lax.rem(u + (hops if d == 0 else NR - hops), NR)

    for hops in range(DIRECT, 0, -1):
        for d in range(2):
            to, send_sem, recv_sem = along(d, hops), hop_send.at[d, hops - 1], z_recv.at[d, hops - 1, h]
            send(remote(mine, zbuf.at[h, u], send_sem.at[0], recv_sem, (to, v, p)))
            send(remote(others, zbuf.at[h, u], send_sem.at[1], recv_sem, (to, mate, p)))
        if hops == DIRECT:
            send(remote(others, zbuf.at[h, u], pair_send, pair_recv, (u, mate, p)))
            send(remote(gt.at[h], gt.at[h], g_send, g_recv, (u, mate, p)))
    for step in range(1, NC // 2):
        to = lax.rem(v + 2 * step, NC)
        send(remote(own, rows.at[v], r_send.at[step], r_recv.at[v], (u, to, p)))
    send(remote(own, rows.at[v], r_send.at[0], r_recv.at[v], (u, mate, p)))
    zbuf[h, u] = own[pl.ds(h * PER_CORE, PER_CORE)]
    rows[v] = own[...]

    for copy in loads[4:]:
        copy.wait()
    scale = weight * (u < NP).astype(F32)
    columns = coup[:, pl.ds(pl.multiple_of(chip * LANES, LANES), LANES)]
    inner = dot(dbk[...], columns)
    inner = jnp.where(h == 0, inner, swap_halves(inner)) * scale
    fixed[...] = dot(coup[pl.ds(part * CHUNK, CHUNK), :], inner, ((0,), (0,)))
    block = jnp.where(h == 0, dak[...], swap_halves(dak[...])) * scale
    fixed[pl.ds(part * CHUNK, CHUNK)] += block

    def arrived(buf, sem):
        remote(buf, buf, pair_send, sem, (u, mate, p)).wait_recv()

    def piece(d, hops, s):
        slot = zbuf.at[s, along(1 - d, hops)]
        arrived(slot, z_recv.at[d, hops - 1, s])
        return slot

    for past in range(DIRECT, NR // 2, DIRECT):
        for s in range(2):
            for d in range(2):
                slot = piece(d, past, s)
                for more in range(min(DIRECT, REACH[d][s] - past), 0, -1):
                    end = past + more - 1
                    send(remote(slot, slot, z_send.at[d, s, end], z_recv.at[d, end, s], (along(d, more), v, p)))
    arrived(zbuf.at[1 - h, u], pair_recv)
    arrived(gt.at[1 - h], g_recv)
    inverse = gt[...].reshape(2 * NR * BLOCK, ROWS).T
    for step in range(1, NC // 2):
        source = lax.rem(v + 2 * step, NC)
        block = rows.at[source]
        arrived(block, r_recv.at[source])
        send(remote(block, block, r_send.at[NC // 2 - 1 + step], r_recv.at[source], (u, mate, p)))
    for step in range(NC // 2):
        source = lax.rem(mate + 2 * step, NC)
        arrived(rows.at[source], r_recv.at[source])
    for a in range(NP):
        turned[a * LANES : (a + 1) * LANES] = rows[:, a].reshape(ROWS, LANES).T
    for hops in range(1, NR // 2 + 1):
        for s in range(2):
            for d in range(2):
                if (hops % DIRECT or hops >= NR // 2) and hops <= REACH[d][s]:
                    piece(d, hops, s)

    for ch in range(PER_CORE):
        gathered = zbuf[:, :, ch].reshape(2 * NR * BLOCK, LANES)
        wsend[ch] = dot(inverse, gathered)
        dest = h * PER_CORE + ch

        @pl.when(dest == v)
        def _():
            wrecv[chip] = wsend[ch]

        @pl.when(dest != v)
        def _():
            remote(wsend.at[ch], wrecv.at[chip], w_send.at[ch], w_recv.at[chip], (u, dest, p)).start()

    for k in range(NC // 2):

        @pl.when(2 * k + v // PER_CORE != v)
        def _():
            arrived(wrecv.at[k], w_recv.at[k])

    both = (wrecv[0] + wrecv[1]) + (wrecv[2] + wrecv[3])
    panel = ((swap_halves(both) - both) * weight).reshape(NC, BLOCK, LANES)
    panel = pack(panel[:, : BLOCK // 2], panel[:, BLOCK // 2 :])
    both = both * weight
    quarter = NP // 2
    terms = []
    for half in range(2):
        out = dot(turned[half * quarter * LANES : (half + 1) * quarter * LANES], both)
        for a in range(half * quarter, (half + 1) * quarter):
            at = (a - half * quarter) * LANES
            top, bottom = out[at : at + CHUNK], out[at + CHUNK : at + LANES]
            terms.append((top, bottom))
            qsend[a, :HALF] = jnp.where(low_lanes((HALF, LANES)), swap_halves(top[:HALF]), top[HALF:])
            qsend[a, HALF:] = panel[a]
            to_me = jnp.logical_and(v == p, a == v)

            @pl.when(to_me)
            def _():
                qrecv[p] = qsend[a]

            @pl.when(jnp.logical_not(to_me))
            def _():
                remote(qsend.at[a], qrecv.at[p], q_send.at[a], q_recv.at[p], (u, a, v)).start()

    for a, (top, bottom) in enumerate(terms):
        first = (top - swap_halves(top)) + swap_halves(bottom) + fixed[a * CHUNK : (a + 1) * CHUNK]
        fsend[a] = pack(first[:HALF], first[HALF:])

        @pl.when(a == p)
        def _():
            frecv[p] = fsend[a]

        @pl.when(a != p)
        def _():
            remote(fsend.at[a], frecv.at[p], f_send.at[a], f_recv.at[p], (u, v, a)).start()

    for q in range(NP):

        @pl.when(q != p)
        def _():
            arrived(frecv.at[q], f_recv.at[q])

        @pl.when(jnp.logical_not(jnp.logical_and(v == p, q == p)))
        def _():
            arrived(qrecv.at[q], q_recv.at[q])

    first, second = frecv[0], qrecv[0]
    for q in range(1, NP):
        first, second = first + frecv[q], second + qrecv[q]
    back = unpack(second[:HALF])
    back = jnp.concatenate([back, back], axis=0).T[:CHUNK]
    total = unpack(first) - back
    tsend[...] = pack(total[:HALF], total[HALF:])
    for step in range(1, NR):
        to = lax.rem(u + step, NR)
        send(remote(tsend, trecv.at[u], t_send.at[step - 1], t_recv.at[u], (to, v, p)))
    trecv[u] = tsend[...]
    panel_ref[...] = unpack(second[HALF:])[:, :CHUNK]

    for step in range(1, NR):
        source = lax.rem(u + step, NR)
        arrived(trecv.at[source], t_recv.at[source])
    total = trecv[0]
    for k in range(1, NR):
        total = total + trecv[k]
    diag_ref[...] = unpack(total)[:, :CHUNK]

    for copy in sent:
        copy.wait_send()
    for ch in range(PER_CORE):

        @pl.when(h * PER_CORE + ch != v)
        def _():
            remote(wsend.at[ch], wsend.at[ch], w_send.at[ch], w_recv.at[0], (u, mate, p)).wait_send()

    for a in range(NP):

        @pl.when(a != p)
        def _():
            remote(fsend.at[a], fsend.at[a], f_send.at[a], f_recv.at[0], (u, mate, p)).wait_send()

        @pl.when(jnp.logical_not(jnp.logical_and(v == p, a == v)))
        def _():
            remote(qsend.at[a], qsend.at[a], q_send.at[a], q_recv.at[0], (u, mate, p)).wait_send()


def shards(
    inverse_grid, factor_b, factor_a, coupling_a, diag_inv_b, diag_inv_a, pole_weights, structure
):
    hbm = pl.BlockSpec(memory_space=pltpu.HBM)
    vmem = pl.BlockSpec(memory_space=pltpu.VMEM)
    dma = pltpu.SemaphoreType.DMA
    panel, diag = pl.pallas_call(
        kernel,
        out_shape=(
            pltpu.VMEM((BLOCK, CHUNK), F32),
            pltpu.VMEM((CHUNK, CHUNK), F32),
        ),
        in_specs=[hbm] * 8,
        out_specs=(vmem, vmem),
        scratch_shapes=[
            pltpu.SMEM((1,), F32),
            pltpu.SMEM((2,), jnp.int32),
            pltpu.VMEM((2, NR * BLOCK, ROWS), F32),
            pltpu.VMEM((BLOCK, WIDTH), F32),
            pltpu.VMEM((BLOCK, WIDTH), F32),
            pltpu.VMEM((WIDTH, WIDTH), F32),
            pltpu.VMEM((CHUNK, WIDTH), F32),
            pltpu.VMEM((CHUNK, LANES), F32),
            pltpu.VMEM((WIDTH, LANES), F32),
            pltpu.VMEM((NC, BLOCK, LANES), F32),
            pltpu.VMEM((2, NR, PER_CORE, BLOCK, LANES), F32),
            pltpu.VMEM((NC, NC, BLOCK, LANES), F32),
            pltpu.VMEM((NP * LANES, ROWS), F32),
            pltpu.VMEM((PER_CORE, ROWS, LANES), F32),
            pltpu.VMEM((NC // 2, ROWS, LANES), F32),
            pltpu.VMEM((NP, HALF, LANES), F32),
            pltpu.VMEM((NP, HALF, LANES), F32),
            pltpu.VMEM((NP, HALF + BLOCK // 2, LANES), F32),
            pltpu.VMEM((NP, HALF + BLOCK // 2, LANES), F32),
            pltpu.VMEM((HALF, LANES), F32),
            pltpu.VMEM((NR, HALF, LANES), F32),
            dma((6,)), dma((2,)), dma, dma, dma((2, 2, NR // 2)), dma((2, NR // 2, 2)), dma((2, DIRECT, 2)), dma, dma,
            dma((NC - 1,)), dma((NC,)), dma((PER_CORE,)), dma((NC // 2,)),
            dma((NP,)), dma((NP,)), dma((NP,)), dma((NP,)), dma((NR - 1,)), dma((NR,)),
        ],
        compiler_params=pltpu.CompilerParams(collective_id=0, has_side_effects=True),
    )(
        inverse_grid[0, 0, :, 0, :].T,
        factor_b[0, 0, 0],
        factor_a[0, 0, 0],
        coupling_a[0],
        diag_inv_b[0],
        diag_inv_a[0],
        pole_weights,
        structure[:, 0, 0],
    )
    return panel[None, None], diag


def solution(mesh):
    in_specs = (
        P("poles", "rows", None, "cols", None),
        P("poles", "rows", "cols", None, None),
        P("poles", "rows", "cols", None, None),
        P("poles", None, None),
        P("poles", None, None),
        P("poles", None, None),
        P("poles"),
        P(None, "rows", "cols"),
    )
    out_specs = (P("rows", "cols", None, "poles"), P("poles", "cols"))
    return jax.shard_map(shards, mesh=mesh, in_specs=in_specs, out_specs=out_specs, check_vma=False)
```

time: 76.1 us -> 63.4 us (0.83)
  the two profiles are of different devices: /device:TPU:51 before, /device:TPU:7 now
where the time goes in v2:
time: 63.4 us; the launch traced here: 63.2 us
  Pallas kernels  60.7 us (96%)
  between operations  1.29 us (2%)
  local copies, waits for them, and re-layouts  1.22 us (2%)
    pallas_call x1, Pallas kernels, shards(): pl.pallas_call(kernel, out_shape=(pltpu.VMEM((BLOCK, CHUNK), F32), pltpu....  60.7 us

profile of v2, /device:TPU:7, one launch (start us, length us, event | category | flops | bytes accessed | tf_op | source)
XLA Modules:
  0.0 63.2 jit_solution(12239704301445338602)
XLA Ops:
  1.3 60.7 %shard_map.95 = (f32[16,64]{1,0:T(8,128)S(1)}, f32[64,64]{1,0:T(8,128)S(1)}) custom-call(f32[192,128]{1,0:T(8,128)} %bitcast.14, f32[16,512]{1,0:T(8,128)} %bitcast.15, f32[16,512]{1,0:T(8,128)} %bitcast.16, f32[512,512]{1,0:T(8,128)} %bitcast.11, f32[512,512]{1,0:T(8,128)} %bitcast.12, f32[512,512]{1,0:T(8,128)} %bitcast.13, f32[1]{0:T(128)S(6)} %copy.14.weight_hbm, ...), custom_call_target="tpu_custom_call" | custom-call | tf_op jit(solution)/shard_map/pallas_call | solution.py:284
  62.0 0.6 copy.12
  62.6 0.6 copy.13

commit v3 on v2

v3 whole, which is shorter than its diff:
```python
import jax
import jax.numpy as jnp
from jax import lax
from jax.experimental import pallas as pl
from jax.experimental.pallas import tpu as pltpu
from jax.sharding import PartitionSpec as P

MESH = pl.DeviceIdType.MESH
F32 = jnp.float32
WIDTH, BLOCK = 512, 16
NR, NC, NP = 12, 8, 8
CHUNK = WIDTH // NP
LANES = 2 * CHUNK
ROWS = NC * BLOCK
HALF = CHUNK // 2
STRIDE = 2
REACH = ((6, 5), (5, 6))
GROUP = NC // 2
FAR_FIRST = sorted(range(1, NR), key=lambda step: -min(step, NR - step))
REACH = ((6, 5), (5, 6))


def dot(left, right, contract=((1,), (0,))):
    return lax.dot_general(
        left, right, (contract, ((), ())), precision=lax.Precision.HIGH, preferred_element_type=F32
    )


def swap_halves(x):
    return pltpu.roll(x, CHUNK, axis=x.ndim - 1)


def low_lanes(shape):
    return lax.broadcasted_iota(jnp.int32, shape, len(shape) - 1) < CHUNK


def pack(top, bottom):
    return jnp.where(low_lanes(top.shape), top, swap_halves(bottom))


def unpack(x):
    return jnp.concatenate([x, swap_halves(x)], axis=0)


def remote(src, dst, send, recv, to):
    return pltpu.make_async_remote_copy(
        src_ref=src, dst_ref=dst, send_sem=send, recv_sem=recv, device_id=to, device_id_type=MESH
    )


def kernel(
    g_hbm, lb_hbm, la_hbm, c_hbm, db_hbm, da_hbm, weight_hbm, keep_hbm,
    panel_ref, diag_ref,
    weight_s, keep_s, gt, lb, la, coup, dbk, dak, fixed, own, zbuf, rows, inverse, turned, terms, panel_out,
    fsend, frecv, qsend, qrecv, tsend, trecv,
    load_sem, late_sem, tile_send, tile_recv, g_send, g_recv, g_pass, z_send, z_pass, z_near, z_far,
    r_send, r_recv, r_pass, f_send, f_recv, q_send, q_recv, t_send, t_recv,
):
    u, v, p = lax.axis_index("rows"), lax.axis_index("cols"), lax.axis_index("poles")
    h, chip = lax.rem(v, 2), v // 2
    mate = chip * 2 + 1 - h
    part = jnp.minimum(u, NP - 1)

    lanes = pl.ds(pl.multiple_of(chip * LANES, LANES), LANES)
    loads = [
        pltpu.make_async_copy(lb_hbm, lb, load_sem.at[0]),
        pltpu.make_async_copy(la_hbm, la, load_sem.at[1]),
        pltpu.make_async_copy(c_hbm, coup, load_sem.at[2]),
        pltpu.make_async_copy(weight_hbm, weight_s, load_sem.at[3]),
        pltpu.make_async_copy(keep_hbm, keep_s, load_sem.at[4]),
    ]
    later = [
        pltpu.make_async_copy(g_hbm, gt.at[v], late_sem.at[0]),
        pltpu.make_async_copy(db_hbm.at[pl.ds(part * CHUNK, CHUNK)], dbk, late_sem.at[1]),
        pltpu.make_async_copy(da_hbm.at[pl.ds(part * CHUNK, CHUNK), lanes], dak, late_sem.at[2]),
    ]
    for copy in loads + later:
        copy.start()

    barrier = pltpu.get_barrier_semaphore()

    def greet(to):
        pl.semaphore_signal(barrier, inc=1, device_id=to, device_id_type=MESH)

    for step in range(1, STRIDE + 1):
        greet((lax.rem(u + step, NR), v, p))
        greet((lax.rem(u + NR - step, NR), v, p))
    for step in range(1, NC):
        greet((u, lax.rem(v + step, NC), p))
        greet((u, v, lax.rem(p + step, NP)))

    for copy in loads:
        copy.wait()
    weight = weight_s[0]
    keep_b = keep_s[0].astype(F32)
    keep_a = keep_s[1].astype(F32)
    panel_a = la[...] * keep_a
    panel_n = dot(lb[...] * keep_b, coup[...])
    for pair in range(NC // 2):
        a, n = (x[:, pair * LANES : (pair + 1) * LANES] for x in (panel_a, panel_n))
        own[2 * pair] = pack(a, n)
        own[2 * pair + 1] = jnp.where(low_lanes(a.shape), swap_halves(a), n)
    pl.semaphore_wait(barrier, 2 * STRIDE + (NC - 1) + (NP - 1))

    def along(d, hops):
        return lax.rem(u + (hops if d == 0 else NR - hops), NR)

    def slot(d, hops):
        return min(2 * hops - 1 + d, NR - 1)

    def arrived(buf, sem):
        remote(buf, buf, tile_send, sem, (u, mate, p)).wait_recv()

    def left(buf, sem):
        remote(buf, buf, sem, tile_recv, (u, mate, p)).wait_send()

    for step in (4, 5, 3, 2, 6, 7, 1):
        to = lax.rem(v + step, NC)
        remote(own.at[to], zbuf.at[0, v], tile_send, tile_recv, (u, to, p)).start()
    zbuf[0, v] = own[v]
    rows[v] = own[...]
    later[0].wait()
    for step in (4, 2, 6):
        remote(gt.at[v], gt.at[v], g_send, g_recv, (u, lax.rem(v + step, NC), p)).start()
    remote(gt.at[v], gt.at[v], g_send, g_pass, (u, mate, p)).start()
    for step in (4, 2, 6):
        remote(own, rows.at[v], r_send, r_recv, (u, lax.rem(v + step, NC), p)).start()
    remote(own, rows.at[v], r_send, r_pass, (u, mate, p)).start()

    for copy in later[1:]:
        copy.wait()
    scale = weight * (u < NP).astype(F32)
    inner = dot(dbk[...], coup[:, lanes])
    inner = jnp.where(h == 0, inner, swap_halves(inner)) * scale
    fixed[...] = dot(coup[pl.ds(part * CHUNK, CHUNK), :], inner, ((0,), (0,)))
    block = jnp.where(h == 0, dak[...], swap_halves(dak[...])) * scale
    fixed[pl.ds(part * CHUNK, CHUNK)] += block

    arrived(zbuf.at[0, : NC - 1], tile_recv)
    for g in range(2):
        piece = pl.ds(g * GROUP, GROUP)
        for d in range(2):
            to = (along(d, STRIDE), v, p)
            remote(zbuf.at[0, piece], zbuf.at[slot(d, STRIDE), piece], z_send, z_pass.at[d, 0, g], to).start()
    for d in range(2):
        remote(zbuf.at[0], zbuf.at[slot(d, 1)], z_send, z_near, (along(d, 1), v, p)).start()
    for level in range(2):
        past = STRIDE * (level + 1)
        for g in range(2):
            piece = pl.ds(g * GROUP, GROUP)
            for d in range(2):
                here = zbuf.at[slot(d, past), piece]
                arrived(here, z_pass.at[d, level, g])
                for more in (2, 1):
                    hops = past + more
                    if hops <= REACH[d][g]:
                        sem = z_near if hops == 3 else z_pass.at[d, 1, g] if hops == 4 else z_far
                        there = zbuf.at[slot(d, hops), piece]
                        remote(here, there, z_send, sem, (along(d, more), v, p)).start()

    arrived(gt.at[:3], g_recv)
    for step in (2, 4, 6):
        block = gt.at[lax.rem(v + step, NC)]
        remote(block, block, g_send, g_pass, (u, mate, p)).start()
    arrived(rows.at[:3], r_recv)
    for step in (2, 4, 6):
        block = rows.at[lax.rem(v + step, NC)]
        remote(block, block, r_send, r_pass, (u, mate, p)).start()
    arrived(gt.at[:4], g_pass)
    for r in range(NR):
        origin = along(r % 2, (r + 1) // 2)
        block = gt[:, pl.ds(pl.multiple_of(origin * BLOCK, BLOCK), BLOCK)]
        inverse[:, r * ROWS : (r + 1) * ROWS] = block.reshape(ROWS, ROWS).T
    arrived(rows.at[:4], r_pass)
    for a in range(NP):
        turned[a * LANES : (a + 1) * LANES] = rows[:, a].reshape(ROWS, LANES).T
    arrived(zbuf.at[:4], z_near)
    split = slot(0, 5)
    both = dot(inverse[:, : split * ROWS], zbuf[:split].reshape(split * ROWS, LANES))
    arrived(zbuf.at[:3], z_far)
    both = both + dot(inverse[:, split * ROWS :], zbuf[split:].reshape((NR - split) * ROWS, LANES))

    panel = ((swap_halves(both) - both) * weight).reshape(NC, BLOCK, LANES)
    panel_out[...] = pack(panel[:, : BLOCK // 2], panel[:, BLOCK // 2 :])
    both = both * weight
    for k in range(NP):
        a = lax.rem(v + NP // 2 + k, NP)
        out = dot(turned[pl.ds(pl.multiple_of(a * LANES, LANES), LANES)], both)
        terms[a] = out
        top = out[:CHUNK]
        qsend[a, :HALF] = jnp.where(low_lanes((HALF, LANES)), swap_halves(top[:HALF]), top[HALF:])
        qsend[a, HALF:] = panel_out[a]
        to_me = jnp.logical_and(v == p, a == v)

        @pl.when(to_me)
        def _():
            qrecv[p] = qsend[a]

        @pl.when(jnp.logical_not(to_me))
        def _():
            remote(qsend.at[a], qrecv.at[p], q_send, q_recv, (u, a, v)).start()

    for k in range(1, NP + 1):
        a = lax.rem(p + k, NP)
        out = terms[a]
        top, bottom = out[:CHUNK], out[CHUNK:]
        own_part = fixed[pl.ds(pl.multiple_of(a * CHUNK, CHUNK), CHUNK)]
        first = (top - swap_halves(top)) + swap_halves(bottom) + own_part
        packed = pack(first[:HALF], first[HALF:])
        if k == NP:
            frecv[p] = packed
        else:
            fsend[a] = packed
            remote(fsend.at[a], frecv.at[p], f_send, f_recv, (u, v, a)).start()

    arrived(frecv.at[: NP - 1], f_recv)

    @pl.when(v == p)
    def _():
        arrived(qrecv.at[: NP - 1], q_recv)

    @pl.when(v != p)
    def _():
        arrived(qrecv, q_recv)

    first, second = frecv[0], qrecv[0]
    for q in range(1, NP):
        first, second = first + frecv[q], second + qrecv[q]
    back = unpack(second[:HALF])
    back = jnp.concatenate([back, back], axis=0).T[:CHUNK]
    total = unpack(first) - back
    tsend[...] = pack(total[:HALF], total[HALF:])
    for step in FAR_FIRST:
        to = lax.rem(u + step, NR)
        remote(tsend, trecv.at[u], t_send, t_recv, (to, v, p)).start()
    trecv[u] = tsend[...]
    panel_ref[...] = unpack(second[HALF:])[:, :CHUNK]

    arrived(trecv.at[: NR - 1], t_recv)
    total = trecv[0]
    for k in range(1, NR):
        total = total + trecv[k]
    diag_ref[...] = unpack(total)[:, :CHUNK]

    left(own.at[: NC - 1], tile_send)
    left(gt.at[: NC - 1], g_send)
    left(rows.at[: NC - 1], r_send)
    left(zbuf.at[: NR - 1], z_send)
    left(fsend.at[: NP - 1], f_send)
    left(trecv.at[: NR - 1], t_send)

    @pl.when(v == p)
    def _():
        left(qsend.at[: NP - 1], q_send)

    @pl.when(v != p)
    def _():
        left(qsend, q_send)


def shards(
    inverse_grid, factor_b, factor_a, coupling_a, diag_inv_b, diag_inv_a, pole_weights, structure
):
    hbm = pl.BlockSpec(memory_space=pltpu.HBM)
    vmem = pl.BlockSpec(memory_space=pltpu.VMEM)
    dma = pltpu.SemaphoreType.DMA
    panel, diag = pl.pallas_call(
        kernel,
        out_shape=(
            pltpu.VMEM((BLOCK, CHUNK), F32),
            pltpu.VMEM((CHUNK, CHUNK), F32),
        ),
        in_specs=[hbm] * 8,
        out_specs=(vmem, vmem),
        scratch_shapes=[
            pltpu.SMEM((1,), F32),
            pltpu.SMEM((2,), jnp.int32),
            pltpu.VMEM((NC, NR * BLOCK, ROWS), F32),
            pltpu.VMEM((BLOCK, WIDTH), F32),
            pltpu.VMEM((BLOCK, WIDTH), F32),
            pltpu.VMEM((WIDTH, WIDTH), F32),
            pltpu.VMEM((CHUNK, WIDTH), F32),
            pltpu.VMEM((CHUNK, LANES), F32),
            pltpu.VMEM((WIDTH, LANES), F32),
            pltpu.VMEM((NC, BLOCK, LANES), F32),
            pltpu.VMEM((NR, NC, BLOCK, LANES), F32),
            pltpu.VMEM((NC, NC, BLOCK, LANES), F32),
            pltpu.VMEM((ROWS, NR * ROWS), F32),
            pltpu.VMEM((NP * LANES, ROWS), F32),
            pltpu.VMEM((NP, LANES, LANES), F32),
            pltpu.VMEM((NC, BLOCK // 2, LANES), F32),
            pltpu.VMEM((NP, HALF, LANES), F32),
            pltpu.VMEM((NP, HALF, LANES), F32),
            pltpu.VMEM((NP, HALF + BLOCK // 2, LANES), F32),
            pltpu.VMEM((NP, HALF + BLOCK // 2, LANES), F32),
            pltpu.VMEM((HALF, LANES), F32),
            pltpu.VMEM((NR, HALF, LANES), F32),
            dma((5,)), dma((3,)), dma, dma, dma, dma, dma, dma, dma((2, 2, 2)), dma, dma,
            dma, dma, dma, dma, dma, dma, dma, dma, dma,
        ],
        compiler_params=pltpu.CompilerParams(collective_id=0, has_side_effects=True),
    )(
        inverse_grid[0, 0, :, 0, :].T,
        factor_b[0, 0, 0],
        factor_a[0, 0, 0],
        coupling_a[0],
        diag_inv_b[0],
        diag_inv_a[0],
        pole_weights,
        structure[:, 0, 0],
    )
    return panel[None, None], diag


def solution(mesh):
    in_specs = (
        P("poles", "rows", None, "cols", None),
        P("poles", "rows", "cols", None, None),
        P("poles", "rows", "cols", None, None),
        P("poles", None, None),
        P("poles", None, None),
        P("poles", None, None),
        P("poles"),
        P(None, "rows", "cols"),
    )
    out_specs = (P("rows", "cols", None, "poles"), P("poles", "cols"))
    return jax.shard_map(shards, mesh=mesh, in_specs=in_specs, out_specs=out_specs, check_vma=False)
```

time: 63.4 us -> 59.5 us (0.938)
  Pallas kernels: 60.7 us -> 56.4 us
    pallas_call x1, Pallas kernels: 60.7 us -> 56.4 us  [shards(): pl.pallas_call(kernel, out_shape=(pltpu.VMEM((BLOCK, CHUNK), F32), pltpu....]
where the time goes in v3:
time: 59.5 us; the launch traced here: 58.9 us
  Pallas kernels  56.4 us (95%)
  between operations  1.29 us (2%)
  local copies, waits for them, and re-layouts  1.22 us (2%)
    pallas_call x1, Pallas kernels, shards(): pl.pallas_call(kernel, out_shape=(pltpu.VMEM((BLOCK, CHUNK), F32), pltpu....  56.4 us
    unnamed x2, local copies, waits for them, and re-layouts  1.22 us

profile of v3, /device:TPU:7, one launch (start us, length us, event | category | flops | bytes accessed | tf_op | source)
XLA Modules:
  0.0 58.9 jit_solution(17287977328828540209)
XLA Ops:
  1.3 56.4 %shard_map.95 = (f32[16,64]{1,0:T(8,128)S(1)}, f32[64,64]{1,0:T(8,128)S(1)}) custom-call(f32[192,128]{1,0:T(8,128)} %bitcast.14, f32[16,512]{1,0:T(8,128)} %bitcast.15, f32[16,512]{1,0:T(8,128)} %bitcast.16, f32[512,512]{1,0:T(8,128)} %bitcast.11, f32[512,512]{1,0:T(8,128)} %bitcast.12, f32[512,512]{1,0:T(8,128)} %bitcast.13, f32[1]{0:T(128)S(6)} %copy.14.weight_hbm, ...), custom_call_target="tpu_custom_call" | custom-call | tf_op jit(solution)/shard_map/pallas_call | solution.py:267
  57.7 0.6 %copy.12 = f32[1,1,16,64]{3,2,1,0:T(8,128)} copy(f32[1,1,16,64]{3,2,1,0:T(8,128)S(1)} %bitcast.10) | data formatting | bytes 8192
  58.3 0.6 %copy.13 = f32[64,64]{1,0:T(8,128)} copy(f32[64,64]{1,0:T(8,128)S(1)} %get-tuple-element.7) | data formatting | bytes 32768

commit v4 on v3

--- a/solution.py
+++ b/solution.py
@@ -15,7 +15,8 @@
 HALF = CHUNK // 2
 STRIDE = 2
 REACH = ((6, 5), (5, 6))
-GROUP = NC // 2
+CHIPS = NC // 2
+NEAREST = (0, 1, 3, 2)
 FAR_FIRST = sorted(range(1, NR), key=lambda step: -min(step, NR - step))
 REACH = ((6, 5), (5, 6))
 
@@ -24,6 +25,11 @@
     return lax.dot_general(
         left, right, (contract, ((), ())), precision=lax.Precision.HIGH, preferred_element_type=F32
     )
+
+
+def halves(x):
+    high = x.astype(jnp.bfloat16)
+    return high, (x - high.astype(F32)).astype(jnp.bfloat16)
 
 
 def swap_halves(x):
@@ -53,8 +59,8 @@
     panel_ref, diag_ref,
     weight_s, keep_s, gt, lb, la, coup, dbk, dak, fixed, own, zbuf, rows, inverse, turned, terms, panel_out,
     fsend, frecv, qsend, qrecv, tsend, trecv,
-    load_sem, late_sem, tile_send, tile_recv, g_send, g_recv, g_pass, z_send, z_pass, z_near, z_far,
-    r_send, r_recv, r_pass, f_send, f_recv, q_send, q_recv, t_send, t_recv,
+    load_sem, late_sem, tile_send, tile_recv, g_send, g_recv, g_opp, g_pass, z_send, z_pass, z_near, z_far, z_last,
+    r_send, r_recv, r_opp, r_pass, f_send, f_recv, q_send, q_recv, t_send, t_recv,
 ):
     u, v, p = lax.axis_index("rows"), lax.axis_index("cols"), lax.axis_index("poles")
     h, chip = lax.rem(v, 2), v // 2
@@ -112,20 +118,32 @@
         remote(buf, buf, tile_send, sem, (u, mate, p)).wait_recv()
 
     def left(buf, sem):
-        remote(buf, buf, sem, tile_recv, (u, mate, p)).wait_send()
-
-    for step in (4, 5, 3, 2, 6, 7, 1):
+        remote(buf, buf, sem, g_recv, (u, mate, p)).wait_send()
+
+    for step in (1, 2, 6, 3, 7, 4, 5):
         to = lax.rem(v + step, NC)
-        remote(own.at[to], zbuf.at[0, v], tile_send, tile_recv, (u, to, p)).start()
+        back = tile_recv.at[lax.rem(chip + CHIPS - to // 2, CHIPS)]
+        remote(own.at[to], zbuf.at[0, v], tile_send, back, (u, to, p)).start()
     zbuf[0, v] = own[v]
     rows[v] = own[...]
     later[0].wait()
-    for step in (4, 2, 6):
+    for step in (2, 6):
         remote(gt.at[v], gt.at[v], g_send, g_recv, (u, lax.rem(v + step, NC), p)).start()
     remote(gt.at[v], gt.at[v], g_send, g_pass, (u, mate, p)).start()
-    for step in (4, 2, 6):
+    for step in (2, 6):
         remote(own, rows.at[v], r_send, r_recv, (u, lax.rem(v + step, NC), p)).start()
     remote(own, rows.at[v], r_send, r_pass, (u, mate, p)).start()
+
+    def tiles(k):
+        return pl.ds(2 * lax.rem(chip + k, CHIPS), 2)
+
+    for k in NEAREST:
+        arrived(zbuf.at[0, : 2 if k else 1], tile_recv.at[k])
+        for hops in (STRIDE, 1):
+            for d in range(2):
+                sem = z_near if hops == 1 else z_pass.at[d, 0, k]
+                to = (along(d, hops), v, p)
+                remote(zbuf.at[0, tiles(k)], zbuf.at[slot(d, hops), tiles(k)], z_send, sem, to).start()
 
     for copy in later[1:]:
         copy.wait()
@@ -136,36 +154,40 @@
     block = jnp.where(h == 0, dak[...], swap_halves(dak[...])) * scale
     fixed[pl.ds(part * CHUNK, CHUNK)] += block
 
-    arrived(zbuf.at[0, : NC - 1], tile_recv)
-    for g in range(2):
-        piece = pl.ds(g * GROUP, GROUP)
-        for d in range(2):
-            to = (along(d, STRIDE), v, p)
-            remote(zbuf.at[0, piece], zbuf.at[slot(d, STRIDE), piece], z_send, z_pass.at[d, 0, g], to).start()
-    for d in range(2):
-        remote(zbuf.at[0], zbuf.at[slot(d, 1)], z_send, z_near, (along(d, 1), v, p)).start()
-    for level in range(2):
+    def relay(level):
         past = STRIDE * (level + 1)
-        for g in range(2):
-            piece = pl.ds(g * GROUP, GROUP)
+        for k in NEAREST:
             for d in range(2):
-                here = zbuf.at[slot(d, past), piece]
-                arrived(here, z_pass.at[d, level, g])
+                here = zbuf.at[slot(d, past), tiles(k)]
+                arrived(here, z_pass.at[d, level, k])
                 for more in (2, 1):
                     hops = past + more
-                    if hops <= REACH[d][g]:
-                        sem = z_near if hops == 3 else z_pass.at[d, 1, g] if hops == 4 else z_far
-                        there = zbuf.at[slot(d, hops), piece]
+                    if hops <= REACH[d][k % 2]:
+                        sem = z_near if hops == 3 else z_pass.at[d, 1, k] if hops == 4 else z_far if hops == 5 else z_last
+                        there = zbuf.at[slot(d, hops), tiles(k)]
                         remote(here, there, z_send, sem, (along(d, more), v, p)).start()
 
-    arrived(gt.at[:3], g_recv)
-    for step in (2, 4, 6):
-        block = gt.at[lax.rem(v + step, NC)]
-        remote(block, block, g_send, g_pass, (u, mate, p)).start()
-    arrived(rows.at[:3], r_recv)
-    for step in (2, 4, 6):
-        block = rows.at[lax.rem(v + step, NC)]
-        remote(block, block, r_send, r_pass, (u, mate, p)).start()
+    def across(buf, send, recv, onward, final):
+        arrived(buf.at[:2], recv)
+        size = buf.shape[1] // 2
+        for half, (source, to) in enumerate(((6, 2), (2, 6))):
+            source = lax.rem(v + source, NC)
+            block = buf.at[source, pl.ds(half * size, size)]
+            remote(block, block, send, onward, (u, lax.rem(v + to, NC), p)).start()
+            remote(buf.at[source], buf.at[source], send, final, (u, mate, p)).start()
+
+    def opposite(buf, send, onward, final):
+        block = buf.at[lax.rem(v + 4, NC)]
+        arrived(block, onward)
+        remote(block, block, send, final, (u, mate, p)).start()
+
+    relay(0)
+    across(gt, g_send, g_recv, g_opp, g_pass)
+    across(rows, r_send, r_recv, r_opp, r_pass)
+    relay(1)
+
+    opposite(gt, g_send, g_opp, g_pass)
+    opposite(rows, r_send, r_opp, r_pass)
     arrived(gt.at[:4], g_pass)
     for r in range(NR):
         origin = along(r % 2, (r + 1) // 2)
@@ -173,21 +195,27 @@
         inverse[:, r * ROWS : (r + 1) * ROWS] = block.reshape(ROWS, ROWS).T
     arrived(rows.at[:4], r_pass)
     for a in range(NP):
-        turned[a * LANES : (a + 1) * LANES] = rows[:, a].reshape(ROWS, LANES).T
+        high, low = halves(rows[:, a].reshape(ROWS, LANES).T)
+        turned[a * LANES : (a + 1) * LANES, :ROWS] = high
+        turned[a * LANES : (a + 1) * LANES, ROWS:] = low
     arrived(zbuf.at[:4], z_near)
-    split = slot(0, 5)
+    split, last = slot(0, 5), slot(0, 6)
     both = dot(inverse[:, : split * ROWS], zbuf[:split].reshape(split * ROWS, LANES))
-    arrived(zbuf.at[:3], z_far)
-    both = both + dot(inverse[:, split * ROWS :], zbuf[split:].reshape((NR - split) * ROWS, LANES))
+    arrived(zbuf.at[:2], z_far)
+    both = both + dot(inverse[:, split * ROWS : last * ROWS], zbuf[split:last].reshape(2 * ROWS, LANES))
+    arrived(zbuf.at[0], z_last)
+    both = both + dot(inverse[:, last * ROWS :], zbuf[last].reshape(ROWS, LANES))
 
     panel = ((swap_halves(both) - both) * weight).reshape(NC, BLOCK, LANES)
     panel_out[...] = pack(panel[:, : BLOCK // 2], panel[:, BLOCK // 2 :])
-    both = both * weight
+    high, low = halves(both * weight)
+    right = jnp.concatenate([high, low], axis=1)
+    right = jnp.concatenate([right, jnp.concatenate([high, jnp.zeros_like(low)], axis=1)], axis=0)
+    out = lax.dot_general(turned[...], right, (((1,), (0,)), ((), ())), preferred_element_type=F32)
+    terms[...] = (out[:, :LANES] + out[:, LANES:]).reshape(NP, LANES, LANES)
     for k in range(NP):
         a = lax.rem(v + NP // 2 + k, NP)
-        out = dot(turned[pl.ds(pl.multiple_of(a * LANES, LANES), LANES)], both)
-        terms[a] = out
-        top = out[:CHUNK]
+        top = terms[a, :CHUNK]
         qsend[a, :HALF] = jnp.where(low_lanes((HALF, LANES)), swap_halves(top[:HALF]), top[HALF:])
         qsend[a, HALF:] = panel_out[a]
         to_me = jnp.logical_and(v == p, a == v)
@@ -286,7 +314,7 @@
             pltpu.VMEM((NR, NC, BLOCK, LANES), F32),
             pltpu.VMEM((NC, NC, BLOCK, LANES), F32),
             pltpu.VMEM((ROWS, NR * ROWS), F32),
-            pltpu.VMEM((NP * LANES, ROWS), F32),
+            pltpu.VMEM((NP * LANES, 2 * ROWS), jnp.bfloat16),
             pltpu.VMEM((NP, LANES, LANES), F32),
             pltpu.VMEM((NC, BLOCK // 2, LANES), F32),
             pltpu.VMEM((NP, HALF, LANES), F32),
@@ -295,7 +323,7 @@
             pltpu.VMEM((NP, HALF + BLOCK // 2, LANES), F32),
             pltpu.VMEM((HALF, LANES), F32),
             pltpu.VMEM((NR, HALF, LANES), F32),
-            dma((5,)), dma((3,)), dma, dma, dma, dma, dma, dma, dma((2, 2, 2)), dma, dma,
+            dma((5,)), dma((3,)), dma, dma((NC // 2,)), dma, dma, dma, dma, dma, dma((2, 2, NC // 2)), dma, dma, dma, dma,
             dma, dma, dma, dma, dma, dma, dma, dma, dma,
         ],
         compiler_params=pltpu.CompilerParams(collective_id=0, has_side_effects=True),

time: 59.5 us -> 56.6 us (0.951)
  Pallas kernels: 56.4 us -> 53.3 us
    pallas_call x1, Pallas kernels: 56.4 us -> 53.3 us  [shards(): pl.pallas_call(kernel, out_shape=(pltpu.VMEM((BLOCK, CHUNK), F32), pltpu....]
where the time goes in v4:
time: 56.6 us; the launch traced here: 55.8 us
  Pallas kernels  53.3 us (94%)
  between operations  1.29 us (2%)
  local copies, waits for them, and re-layouts  1.22 us (2%)
    pallas_call x1, Pallas kernels, shards(): pl.pallas_call(kernel, out_shape=(pltpu.VMEM((BLOCK, CHUNK), F32), pltpu....  53.3 us
    unnamed x2, local copies, waits for them, and re-layouts  1.22 us

profile of v4, /device:TPU:7, one launch (start us, length us, event | category | flops | bytes accessed | tf_op | source)
XLA Modules:
  0.0 55.8 jit_solution(7248938015766242543)
XLA Ops:
  1.3 53.3 %shard_map.95 = (f32[16,64]{1,0:T(8,128)S(1)}, f32[64,64]{1,0:T(8,128)S(1)}) custom-call(f32[192,128]{1,0:T(8,128)} %bitcast.14, f32[16,512]{1,0:T(8,128)} %bitcast.15, f32[16,512]{1,0:T(8,128)} %bitcast.16, f32[512,512]{1,0:T(8,128)} %bitcast.11, f32[512,512]{1,0:T(8,128)} %bitcast.12, f32[512,512]{1,0:T(8,128)} %bitcast.13, f32[1]{0:T(128)S(6)} %copy.14.weight_hbm, ...), custom_call_target="tpu_custom_call" | custom-call | tf_op jit(solution)/shard_map/pallas_call | solution.py:295
  54.5 0.6 %copy.12 = f32[1,1,16,64]{3,2,1,0:T(8,128)} copy(f32[1,1,16,64]{3,2,1,0:T(8,128)S(1)} %bitcast.10) | data formatting | bytes 8192
  55.1 0.6 %copy.13 = f32[64,64]{1,0:T(8,128)} copy(f32[64,64]{1,0:T(8,128)S(1)} %get-tuple-element.7) | data formatting | bytes 32768

commit v5 on v4

--- a/solution.py
+++ b/solution.py
@@ -59,7 +59,7 @@
     panel_ref, diag_ref,
     weight_s, keep_s, gt, lb, la, coup, dbk, dak, fixed, own, zbuf, rows, inverse, turned, terms, panel_out,
     fsend, frecv, qsend, qrecv, tsend, trecv,
-    load_sem, late_sem, tile_send, tile_recv, g_send, g_recv, g_opp, g_pass, z_send, z_pass, z_near, z_far, z_last,
+    load_sem, late_sem, tile_send, tile_recv, g_send, g_recv, g_opp, g_pass, z_send, z_pass, z_rest, g_last,
     r_send, r_recv, r_opp, r_pass, f_send, f_recv, q_send, q_recv, t_send, t_recv,
 ):
     u, v, p = lax.axis_index("rows"), lax.axis_index("cols"), lax.axis_index("poles")
@@ -88,12 +88,13 @@
     def greet(to):
         pl.semaphore_signal(barrier, inc=1, device_id=to, device_id_type=MESH)
 
+    for step in (4, 5, 3, 2, 6, 7, 1):
+        greet((u, lax.rem(v + step, NC), p))
+    for step in range(1, NP):
+        greet((u, v, lax.rem(p + step, NP)))
     for step in range(1, STRIDE + 1):
         greet((lax.rem(u + step, NR), v, p))
         greet((lax.rem(u + NR - step, NR), v, p))
-    for step in range(1, NC):
-        greet((u, lax.rem(v + step, NC), p))
-        greet((u, v, lax.rem(p + step, NP)))
 
     for copy in loads:
         copy.wait()
@@ -141,7 +142,7 @@
         arrived(zbuf.at[0, : 2 if k else 1], tile_recv.at[k])
         for hops in (STRIDE, 1):
             for d in range(2):
-                sem = z_near if hops == 1 else z_pass.at[d, 0, k]
+                sem = z_rest.at[k] if hops == 1 else z_pass.at[d, 0, k]
                 to = (along(d, hops), v, p)
                 remote(zbuf.at[0, tiles(k)], zbuf.at[slot(d, hops), tiles(k)], z_send, sem, to).start()
 
@@ -163,7 +164,7 @@
                 for more in (2, 1):
                     hops = past + more
                     if hops <= REACH[d][k % 2]:
-                        sem = z_near if hops == 3 else z_pass.at[d, 1, k] if hops == 4 else z_far if hops == 5 else z_last
+                        sem = z_pass.at[d, 1, k] if hops == 4 else z_rest.at[k]
                         there = zbuf.at[slot(d, hops), tiles(k)]
                         remote(here, there, z_send, sem, (along(d, more), v, p)).start()
 
@@ -186,47 +187,60 @@
     across(rows, r_send, r_recv, r_opp, r_pass)
     relay(1)
 
-    opposite(gt, g_send, g_opp, g_pass)
+    def share(k):
+        parts = []
+        for r in range(NR):
+            origin = along(r % 2, (r + 1) // 2)
+            at = pl.ds(pl.multiple_of(origin * BLOCK, BLOCK), BLOCK)
+            parts.append(gt[tiles(k), at].reshape(2 * BLOCK, ROWS))
+        inverse[k] = jnp.concatenate(parts, axis=0).T
+
+    def column_sum(k):
+        arrived(zbuf.at[: NR // 2 + 1, :2], z_rest.at[k])
+        return dot(inverse[k], zbuf[:, tiles(k)].reshape(2 * NR * BLOCK, LANES))
+
+    arrived(gt.at[:3], g_pass)
+    for k in NEAREST[:3]:
+        share(k)
+    opposite(gt, g_send, g_opp, g_last)
     opposite(rows, r_send, r_opp, r_pass)
-    arrived(gt.at[:4], g_pass)
-    for r in range(NR):
-        origin = along(r % 2, (r + 1) // 2)
-        block = gt[:, pl.ds(pl.multiple_of(origin * BLOCK, BLOCK), BLOCK)]
-        inverse[:, r * ROWS : (r + 1) * ROWS] = block.reshape(ROWS, ROWS).T
+    both = column_sum(NEAREST[0])
+    for k in NEAREST[1:3]:
+        both = both + column_sum(k)
+    arrived(gt.at[0], g_last)
+    share(NEAREST[3])
+    both = both + column_sum(NEAREST[3])
     arrived(rows.at[:4], r_pass)
     for a in range(NP):
         high, low = halves(rows[:, a].reshape(ROWS, LANES).T)
         turned[a * LANES : (a + 1) * LANES, :ROWS] = high
         turned[a * LANES : (a + 1) * LANES, ROWS:] = low
-    arrived(zbuf.at[:4], z_near)
-    split, last = slot(0, 5), slot(0, 6)
-    both = dot(inverse[:, : split * ROWS], zbuf[:split].reshape(split * ROWS, LANES))
-    arrived(zbuf.at[:2], z_far)
-    both = both + dot(inverse[:, split * ROWS : last * ROWS], zbuf[split:last].reshape(2 * ROWS, LANES))
-    arrived(zbuf.at[0], z_last)
-    both = both + dot(inverse[:, last * ROWS :], zbuf[last].reshape(ROWS, LANES))
 
     panel = ((swap_halves(both) - both) * weight).reshape(NC, BLOCK, LANES)
     panel_out[...] = pack(panel[:, : BLOCK // 2], panel[:, BLOCK // 2 :])
     high, low = halves(both * weight)
     right = jnp.concatenate([high, low], axis=1)
     right = jnp.concatenate([right, jnp.concatenate([high, jnp.zeros_like(low)], axis=1)], axis=0)
-    out = lax.dot_general(turned[...], right, (((1,), (0,)), ((), ())), preferred_element_type=F32)
-    terms[...] = (out[:, :LANES] + out[:, LANES:]).reshape(NP, LANES, LANES)
-    for k in range(NP):
-        a = lax.rem(v + NP // 2 + k, NP)
-        top = terms[a, :CHUNK]
-        qsend[a, :HALF] = jnp.where(low_lanes((HALF, LANES)), swap_halves(top[:HALF]), top[HALF:])
-        qsend[a, HALF:] = panel_out[a]
-        to_me = jnp.logical_and(v == p, a == v)
-
-        @pl.when(to_me)
-        def _():
-            qrecv[p] = qsend[a]
-
-        @pl.when(jnp.logical_not(to_me))
-        def _():
-            remote(qsend.at[a], qrecv.at[p], q_send, q_recv, (u, a, v)).start()
+    half = NP // 2
+    for part in range(2):
+        begin = half * lax.rem(v // half + 1 + part, 2)
+        lhs = turned[pl.ds(pl.multiple_of(begin * LANES, half * LANES), half * LANES)]
+        out = lax.dot_general(lhs, right, (((1,), (0,)), ((), ())), preferred_element_type=F32)
+        out = (out[:, :LANES] + out[:, LANES:]).reshape(half, LANES, LANES)
+        terms[pl.ds(begin, half)] = out
+        for k in range(half):
+            a, top = begin + k, out[k, :CHUNK]
+            qsend[a, :HALF] = jnp.where(low_lanes((HALF, LANES)), swap_halves(top[:HALF]), top[HALF:])
+            qsend[a, HALF:] = panel_out[a]
+            to_me = jnp.logical_and(v == p, a == v)
+
+            @pl.when(to_me)
+            def _():
+                qrecv[p] = qsend[a]
+
+            @pl.when(jnp.logical_not(to_me))
+            def _():
+                remote(qsend.at[a], qrecv.at[p], q_send, q_recv, (u, a, v)).start()
 
     for k in range(1, NP + 1):
         a = lax.rem(p + k, NP)
@@ -313,7 +327,7 @@
             pltpu.VMEM((NC, BLOCK, LANES), F32),
             pltpu.VMEM((NR, NC, BLOCK, LANES), F32),
             pltpu.VMEM((NC, NC, BLOCK, LANES), F32),
-            pltpu.VMEM((ROWS, NR * ROWS), F32),
+            pltpu.VMEM((CHIPS, ROWS, 2 * NR * BLOCK), F32),
             pltpu.VMEM((NP * LANES, 2 * ROWS), jnp.bfloat16),
             pltpu.VMEM((NP, LANES, LANES), F32),
             pltpu.VMEM((NC, BLOCK // 2, LANES), F32),
@@ -323,7 +337,7 @@
             pltpu.VMEM((NP, HALF + BLOCK // 2, LANES), F32),
             pltpu.VMEM((HALF, LANES), F32),
             pltpu.VMEM((NR, HALF, LANES), F32),
-            dma((5,)), dma((3,)), dma, dma((NC // 2,)), dma, dma, dma, dma, dma, dma((2, 2, NC // 2)), dma, dma, dma, dma,
+            dma((5,)), dma((3,)), dma, dma((NC // 2,)), dma, dma, dma, dma, dma, dma((2, 2, NC // 2)), dma((NC // 2,)), dma, dma,
             dma, dma, dma, dma, dma, dma, dma, dma, dma,
         ],
         compiler_params=pltpu.CompilerParams(collective_id=0, has_side_effects=True),

time: 56.6 us -> 55.3 us (0.977)
  Pallas kernels: 53.3 us -> 52.3 us
    pallas_call x1, Pallas kernels: 53.3 us -> 52.3 us  [shards(): pl.pallas_call(kernel, out_shape=(pltpu.VMEM((BLOCK, CHUNK), F32), pltpu....]
where the time goes in v5:
time: 55.3 us; the launch traced here: 54.8 us
  Pallas kernels  52.3 us (95%)
  between operations  1.29 us (2%)
  local copies, waits for them, and re-layouts  1.22 us (2%)
    pallas_call x1, Pallas kernels, shards(): pl.pallas_call(kernel, out_shape=(pltpu.VMEM((BLOCK, CHUNK), F32), pltpu....  52.3 us
    unnamed x2, local copies, waits for them, and re-layouts  1.22 us

profile of v5, /device:TPU:7, one launch (start us, length us, event | category | flops | bytes accessed | tf_op | source)
XLA Modules:
  0.0 54.8 jit_solution(3077027026517115926)
XLA Ops:
  1.3 52.3 %shard_map.95 = (f32[16,64]{1,0:T(8,128)S(1)}, f32[64,64]{1,0:T(8,128)S(1)}) custom-call(f32[192,128]{1,0:T(8,128)} %bitcast.14, f32[16,512]{1,0:T(8,128)} %bitcast.15, f32[16,512]{1,0:T(8,128)} %bitcast.16, f32[512,512]{1,0:T(8,128)} %bitcast.11, f32[512,512]{1,0:T(8,128)} %bitcast.12, f32[512,512]{1,0:T(8,128)} %bitcast.13, f32[1]{0:T(128)S(6)} %copy.14.weight_hbm, ...), custom_call_target="tpu_custom_call" | custom-call | tf_op jit(solution)/shard_map/pallas_call | solution.py:309
  53.5 0.6 %copy.12 = f32[1,1,16,64]{3,2,1,0:T(8,128)} copy(f32[1,1,16,64]{3,2,1,0:T(8,128)S(1)} %bitcast.10) | data formatting | bytes 8192
  54.1 0.6 %copy.13 = f32[64,64]{1,0:T(8,128)} copy(f32[64,64]{1,0:T(8,128)S(1)} %get-tuple-element.7) | data formatting | bytes 32768

commit v6 on v5

--- a/solution.py
+++ b/solution.py
@@ -57,10 +57,10 @@
 def kernel(
     g_hbm, lb_hbm, la_hbm, c_hbm, db_hbm, da_hbm, weight_hbm, keep_hbm,
     panel_ref, diag_ref,
-    weight_s, keep_s, gt, lb, la, coup, dbk, dak, fixed, own, zbuf, rows, inverse, turned, terms, panel_out,
+    weight_s, keep_s, gt, lb, la, coup, dbk, dak, fixed, own, zbuf, rows, inverse, turned, panel_out, panel_in,
     fsend, frecv, qsend, qrecv, tsend, trecv,
     load_sem, late_sem, tile_send, tile_recv, g_send, g_recv, g_opp, g_pass, z_send, z_pass, z_rest, g_last,
-    r_send, r_recv, r_opp, r_pass, f_send, f_recv, q_send, q_recv, t_send, t_recv,
+    r_send, r_recv, r_opp, r_pass, f_send, f_recv, q_send, q_recv, t_send, t_recv, n_send, n_recv,
 ):
     u, v, p = lax.axis_index("rows"), lax.axis_index("cols"), lax.axis_index("poles")
     h, chip = lax.rem(v, 2), v // 2
@@ -227,11 +227,9 @@
         lhs = turned[pl.ds(pl.multiple_of(begin * LANES, half * LANES), half * LANES)]
         out = lax.dot_general(lhs, right, (((1,), (0,)), ((), ())), preferred_element_type=F32)
         out = (out[:, :LANES] + out[:, LANES:]).reshape(half, LANES, LANES)
-        terms[pl.ds(begin, half)] = out
         for k in range(half):
             a, top = begin + k, out[k, :CHUNK]
-            qsend[a, :HALF] = jnp.where(low_lanes((HALF, LANES)), swap_halves(top[:HALF]), top[HALF:])
-            qsend[a, HALF:] = panel_out[a]
+            qsend[a] = jnp.where(low_lanes((HALF, LANES)), swap_halves(top[:HALF]), top[HALF:])
             to_me = jnp.logical_and(v == p, a == v)
 
             @pl.when(to_me)
@@ -242,18 +240,26 @@
             def _():
                 remote(qsend.at[a], qrecv.at[p], q_send, q_recv, (u, a, v)).start()
 
-    for k in range(1, NP + 1):
-        a = lax.rem(p + k, NP)
-        out = terms[a]
-        top, bottom = out[:CHUNK], out[CHUNK:]
-        own_part = fixed[pl.ds(pl.multiple_of(a * CHUNK, CHUNK), CHUNK)]
-        first = (top - swap_halves(top)) + swap_halves(bottom) + own_part
-        packed = pack(first[:HALF], first[HALF:])
-        if k == NP:
-            frecv[p] = packed
-        else:
-            fsend[a] = packed
-            remote(fsend.at[a], frecv.at[p], f_send, f_recv, (u, v, a)).start()
+        for k in range(half):
+            a, top, bottom = begin + k, out[k, :CHUNK], out[k, CHUNK:]
+            own_part = fixed[pl.ds(pl.multiple_of(a * CHUNK, CHUNK), CHUNK)]
+            first = top + swap_halves(bottom - top) + own_part
+            fsend[a] = pack(first[:HALF], first[HALF:])
+
+    frecv[p] = fsend[p]
+    for step in range(1, NP):
+        a = lax.rem(p + step, NP)
+        remote(fsend.at[a], frecv.at[p], f_send, f_recv, (u, v, a)).start()
+    for a in range(NC):
+        to_me = jnp.logical_and(v == p, a == v)
+
+        @pl.when(to_me)
+        def _():
+            panel_in[p] = panel_out[a]
+
+        @pl.when(jnp.logical_not(to_me))
+        def _():
+            remote(panel_out.at[a], panel_in.at[p], n_send, n_recv, (u, a, v)).start()
 
     arrived(frecv.at[: NP - 1], f_recv)
 
@@ -268,7 +274,7 @@
     first, second = frecv[0], qrecv[0]
     for q in range(1, NP):
         first, second = first + frecv[q], second + qrecv[q]
-    back = unpack(second[:HALF])
+    back = unpack(second)
     back = jnp.concatenate([back, back], axis=0).T[:CHUNK]
     total = unpack(first) - back
     tsend[...] = pack(total[:HALF], total[HALF:])
@@ -276,7 +282,19 @@
         to = lax.rem(u + step, NR)
         remote(tsend, trecv.at[u], t_send, t_recv, (to, v, p)).start()
     trecv[u] = tsend[...]
-    panel_ref[...] = unpack(second[HALF:])[:, :CHUNK]
+
+    @pl.when(v == p)
+    def _():
+        arrived(panel_in.at[: NP - 1], n_recv)
+
+    @pl.when(v != p)
+    def _():
+        arrived(panel_in, n_recv)
+
+    total = panel_in[0]
+    for k in range(1, NP):
+        total = total + panel_in[k]
+    panel_ref[...] = unpack(total)[:, :CHUNK]
 
     arrived(trecv.at[: NR - 1], t_recv)
     total = trecv[0]
@@ -294,10 +312,12 @@
     @pl.when(v == p)
     def _():
         left(qsend.at[: NP - 1], q_send)
+        left(panel_out.at[: NC - 1], n_send)
 
     @pl.when(v != p)
     def _():
         left(qsend, q_send)
+        left(panel_out, n_send)
 
 
 def shards(
@@ -329,16 +349,16 @@
             pltpu.VMEM((NC, NC, BLOCK, LANES), F32),
             pltpu.VMEM((CHIPS, ROWS, 2 * NR * BLOCK), F32),
             pltpu.VMEM((NP * LANES, 2 * ROWS), jnp.bfloat16),
-            pltpu.VMEM((NP, LANES, LANES), F32),
             pltpu.VMEM((NC, BLOCK // 2, LANES), F32),
+            pltpu.VMEM((NP, BLOCK // 2, LANES), F32),
             pltpu.VMEM((NP, HALF, LANES), F32),
             pltpu.VMEM((NP, HALF, LANES), F32),
-            pltpu.VMEM((NP, HALF + BLOCK // 2, LANES), F32),
-            pltpu.VMEM((NP, HALF + BLOCK // 2, LANES), F32),
+            pltpu.VMEM((NP, HALF, LANES), F32),
+            pltpu.VMEM((NP, HALF, LANES), F32),
             pltpu.VMEM((HALF, LANES), F32),
             pltpu.VMEM((NR, HALF, LANES), F32),
             dma((5,)), dma((3,)), dma, dma((NC // 2,)), dma, dma, dma, dma, dma, dma((2, 2, NC // 2)), dma((NC // 2,)), dma, dma,
-            dma, dma, dma, dma, dma, dma, dma, dma, dma,
+            dma, dma, dma, dma, dma, dma, dma, dma, dma, dma, dma,
         ],
         compiler_params=pltpu.CompilerParams(collective_id=0, has_side_effects=True),
     )(

time: 55.3 us -> 55.1 us (level)
  no operation moved by 1% of the time
where the time goes in v6:
time: 55.1 us; the launch traced here: 54.5 us
  Pallas kernels  52 us (94%)
  between operations  1.29 us (2%)
  local copies, waits for them, and re-layouts  1.22 us (2%)
    pallas_call x1, Pallas kernels, shards(): pl.pallas_call(kernel, out_shape=(pltpu.VMEM((BLOCK, CHUNK), F32), pltpu....  52 us
    unnamed x2, local copies, waits for them, and re-layouts  1.22 us

profile of v6, /device:TPU:7, one launch (start us, length us, event | category | flops | bytes accessed | tf_op | source)
XLA Modules:
  0.0 54.5 jit_solution(3548538105269769415)
XLA Ops:
  1.3 52.0 %shard_map.95 = (f32[16,64]{1,0:T(8,128)S(1)}, f32[64,64]{1,0:T(8,128)S(1)}) custom-call(f32[192,128]{1,0:T(8,128)} %bitcast.14, f32[16,512]{1,0:T(8,128)} %bitcast.15, f32[16,512]{1,0:T(8,128)} %bitcast.16, f32[512,512]{1,0:T(8,128)} %bitcast.11, f32[512,512]{1,0:T(8,128)} %bitcast.12, f32[512,512]{1,0:T(8,128)} %bitcast.13, f32[1]{0:T(128)S(6)} %copy.14.weight_hbm, ...), custom_call_target="tpu_custom_call" | custom-call | tf_op jit(solution)/shard_map/pallas_call | solution.py:329
  53.3 0.6 %copy.12 = f32[1,1,16,64]{3,2,1,0:T(8,128)} copy(f32[1,1,16,64]{3,2,1,0:T(8,128)S(1)} %bitcast.10) | data formatting | bytes 8192
  53.9 0.6 %copy.13 = f32[64,64]{1,0:T(8,128)} copy(f32[64,64]{1,0:T(8,128)S(1)} %get-tuple-element.7) | data formatting | bytes 32768
